TPU v7x, 256 devices: a whole 4x4x8 slice. The times are simulated.
256 devices in a mesh: freq: 16 (over z, core), tile: 16 (over y, x).
Axes of the slice: x: 4, y: 4, z: 8, core: 2. Of those that a mesh axis runs over, the one named last changes fastest.
Arguments:
- focal_field: bfloat16 [16, 16384, 2, 256], P('freq', 'tile'), may hold values from -6 to 6
- v_factors: bfloat16 [16, 16, 16384, 128], P('freq', None, 'tile'), may hold values from -0.1875 to 0.1875
- u_factors: bfloat16 [16, 16384, 16, 128], P('freq', 'tile'), may hold values from -0.125 to 0.125
- ranks: int32 [16, 16, 16], P('freq', None, 'tile'), may hold values from 16 to 64, as said below
- tile_mask: int32 [16, 16, 16], P('freq', None, 'tile'), may hold values 0 or 1
- initial_focus: bfloat16 [16, 32, 1024, 256], P('tile', None, 'freq'), may hold values from -6 to 6
- mute_starts: int32 [16, 1024, 256], P('tile', 'freq'), may hold values from 1 to 31
- taper: float32 [16, 1024], P('tile', 'freq'), may hold values from 0.3 to 3
Outputs:
- focusing: bfloat16 [16, 32, 1024, 256], P('tile', None, 'freq')
- correlation: float32 [16, 256, 256], P('freq', 'tile')
Inputs may be any that keep to these rules, and one draw needn't show every extreme that they name: `ranks`: in every frequency some tile has rank exactly 64; no rank is below 16.
All inputs are finite; a program needn't handle non-finite values. No bound on the sum of `tile_mask` on one device may be relied on, other than what follows from the above.
Results may differ from a plain program's by a relative error of at most 0.009.
Values may be sent and summed in bfloat16 or wider, within the bound.
No kernel may reach another device: no remote copies, remote signals or barrier semaphores. Data moves between devices by JAX's collectives and lax.ppermute only.
A program may use at most 64 MiB of HBM per device.

v0:
```python
import math

import jax
import jax.numpy as jnp
from jax import lax
from jax.sharding import PartitionSpec as P


def dft_table(trace_length, freq_count):
    clock_moments = jnp.arange(trace_length, dtype=jnp.float32)
    angular_rate = jnp.arange(freq_count, dtype=jnp.float32) + 1.0
    rotation_radians = 2.0 * math.pi / trace_length * clock_moments[:, None] * angular_rate[None, :]
    return jnp.stack([jnp.cos(rotation_radians), -jnp.sin(rotation_radians)], axis=2) / jnp.sqrt(
        jnp.float32(freq_count)
    )


def stacked_rhs(received):
    sources = received.shape[0]
    columns = received.shape[3]
    real_c = received[:, :, 0, :]
    imag_c = received[:, :, 1, :]
    upper = jnp.concatenate([real_c, -imag_c], axis=1)
    lower = jnp.concatenate([imag_c, real_c], axis=1)
    return jnp.concatenate([upper, lower], axis=2).reshape(sources * upper.shape[1], 2 * columns)


def body(focal_field, v_factors, u_factors, ranks, tile_mask, initial_focus, mute_starts, taper):
    tile_count = lax.axis_size("tile")
    rank_max = v_factors.shape[3] // 2
    focal_count = focal_field.shape[3]
    tile_rows = focal_field.shape[1]
    flat_field = focal_field[0].reshape(tile_rows, 2 * focal_count)
    moments = jnp.einsum(
        "irk,rc->ikc", v_factors[0], flat_field, preferred_element_type=jnp.float32
    )
    real_part = moments[:, :rank_max, :focal_count] - moments[:, rank_max:, focal_count:]
    imag_part = moments[:, :rank_max, focal_count:] + moments[:, rank_max:, :focal_count]
    levels = jnp.arange(rank_max, dtype=jnp.int32)
    retained = (
        (levels[None, :] < ranks[0, :, 0][:, None]) & (tile_mask[0, :, 0][:, None] > 0)
    ).astype(jnp.float32)
    coeffs = jnp.stack(
        [real_part * retained[:, :, None], imag_part * retained[:, :, None]], axis=2
    ).astype(jnp.bfloat16)
    u_rows = u_factors[0]
    received = lax.all_to_all(coeffs, "tile", split_axis=0, concat_axis=0, tiled=True)
    columns = received.shape[3]
    product = jnp.dot(
        u_rows.reshape(tile_rows, -1), stacked_rhs(received), preferred_element_type=jnp.float32
    )
    fields = product.reshape(tile_rows, 2, columns).astype(jnp.bfloat16)
    trace_length = initial_focus.shape[1]
    gathered = lax.all_to_all(fields[None], "freq", split_axis=1, concat_axis=0, tiled=True)
    dft_weights = dft_table(trace_length, gathered.shape[0])
    trace_signal = jnp.einsum(
        "tfc,fscn->tsn", dft_weights, gathered.astype(jnp.float32), precision=lax.Precision.HIGHEST
    )
    group_rows = trace_signal.shape[1]
    clock_moments = jnp.arange(trace_length, dtype=jnp.int32)
    silenced_wavefield = jnp.where(
        clock_moments[:, None, None] < mute_starts[0][None, :, :], trace_signal, 0.0
    )
    focusing = (initial_focus[0].astype(jnp.float32) - silenced_wavefield).astype(jnp.bfloat16)
    weighted = (focusing.astype(jnp.float32) * taper[0][None, :, None]).astype(jnp.bfloat16)
    flat_focus = focusing.reshape(trace_length * group_rows, focal_count)
    flat_weighted = weighted.reshape(trace_length * group_rows, focal_count)
    partial_value = lax.dot_general(
        flat_focus, flat_weighted, (((0,), (0,)), ((), ())), preferred_element_type=jnp.float32
    )
    normalizer = 1.0 / float(tile_count * trace_length * group_rows)
    summed_total = lax.psum(partial_value.astype(jnp.bfloat16), "tile").astype(jnp.float32)
    share_rows = focal_count // tile_count
    own_rows = lax.dynamic_slice_in_dim(
        summed_total, lax.axis_index("tile") * share_rows, share_rows, 0
    )
    return (focusing[None], (own_rows * normalizer)[None])


def solution(mesh):
    placed = (
        P("freq", "tile", None, None),
        P("freq", None, "tile", None),
        P("freq", "tile", None, None),
        P("freq", None, "tile"),
        P("freq", None, "tile"),
        P("tile", None, "freq", None),
        P("tile", "freq", None),
        P("tile", "freq"),
    )
    return jax.shard_map(
        body,
        mesh=mesh,
        in_specs=placed,
        out_specs=(P("tile", None, "freq", None), P("freq", "tile", None)),
        check_vma=False,
    )
```

profile of v0, /device:TPU:1, one launch (start us, length us, event | category | flops | bytes accessed | tf_op | source)
XLA Modules:
  0.0 179.2 jit_solution(2746314441526483126)
XLA Ops:
  7.2 0.0 copy-start.5
  7.2 1.7 reshape.179
  8.9 0.0 copy-done.5
  8.9 0.0 copy-start.1
  9.0 4.6 %fusion.3 = f32[16,128,512]{2,1,0:T(8,128)S(1)} fusion(bf16[1024,512,1]{1,0,2:T(8,128)(2,1)S(1)} %reshape.179, bf16[1,16,1024,128]{3,2,1,0:T(8,128)(2,1)} %param.9), kind=kOutput, calls=%fused_computation.3 | convolution fusion | flops 2147483648 | bytes 9437184 | tf_op jit(solution)/shard_map/irk,rc->ikc/dot_general | solution.py:34
  13.5 0.0 copy-done.1
  13.6 0.1 fusion.27
  13.6 0.4 fusion.18
  14.0 0.1 pad_maximum_fusion
  14.1 0.1 copy.24
  14.2 23.4 %all_to_all.17 = bf16[16,64,2,256]{3,1,2,0:T(8,128)(2,1)S(1)} all-to-all(bf16[16,64,2,256]{3,1,2,0:T(8,128)(2,1)S(1)} %copy.24), channel_id=1, replica_groups=mesh['freq'=16,'tile'=16] {'tile'}, dimensions={0} | all-to-all | bytes 2097152 | tf_op jit(solution)/shard_map/all_to_all | solution.py:47
  37.6 0.1 slice_bitcast_fusion
  37.7 0.0 copy-start.2
  37.8 0.2 maximum_maximum_fusion
  38.0 1.9 %copy-done.2 = bf16[1,1024,16,128]{3,2,1,0:T(8,128)(2,1)S(1)} copy-done((bf16[1,1024,16,128]{3,2,1,0:T(8,128)(2,1)S(1)}, bf16[1,1024,16,128]{3,2,1,0:T(8,128)(2,1)}, u32[]{:S(2)}) %copy-start.2) | copy-done | bytes 4194328
  39.9 2.4 %fusion.7 = bf16[512,1024]{1,0:T(8,128)(2,1)S(1)} fusion(bf16[2048,512]{1,0:T(8,128)(2,1)S(1)} %bitcast.54, bf16[128,8,16,128]{3,2,1,0:T(8,128)(2,1)S(1)} %bitcast.59), kind=kOutput, calls=%fused_computation.12 | convolution fusion | flops 2148007936 | bytes 7340032 | tf_op jit(solution)/shard_map/dot_general | solution.py:49
  42.3 0.0 copy-start.3
  42.3 0.0 copy-start.4
  42.4 2.0 %copy.26 = bf16[1,1024,2,256]{3,2,0,1:T(2,128)(2,1)} copy(bf16[1,1024,2,256]{1,3,2,0:T(8,128)(2,1)S(1)} %bitcast.56) | data formatting | bytes 2097152 | tf_op jit(solution)/shard_map/convert_element_type | solution.py:52
  44.4 10.5 %all-to-all-start.1 = ((bf16[1,1024,2,256]{3,2,0,1:T(2,128)(2,1)}), bf16[1,1024,2,256]{3,2,0,1:T(2,128)(2,1)S(1)}, u32[]{:S(2)}, u32[]{:S(2)}) async-start(bf16[1,1024,2,256]{3,2,0,1:T(2,128)(2,1)} %copy.26), calls=%async_computation.1 | async-start | bytes 2097152 | tf_op jit(solution)/shard_map/all_to_all | solution.py:54
  54.9 0.0 copy-start
  54.9 0.0 all-reduce.2.cloned.1.call-start
  55.0 0.1 multiply_cosine_fusion
  55.1 27.8 %all-to-all-done.1 = bf16[1,1024,2,256]{3,2,0,1:T(2,128)(2,1)S(1)} async-done(((bf16[1,1024,2,256]{3,2,0,1:T(2,128)(2,1)}), bf16[1,1024,2,256]{3,2,0,1:T(2,128)(2,1)S(1)}, u32[]{:S(2)}, u32[]{:S(2)}) %all-to-all-start.1) | async-done | bytes 1048608 | tf_op jit(solution)/shard_map/all_to_all | solution.py:54
  82.9 0.0 copy-done.3
  82.9 0.0 copy-done.4
  82.9 1.9 %fusion.5 = bf16[32,64,256]{2,0,1:T(8,128)(2,1)S(1)} fusion(bf16[16,64,2,256]{3,2,1,0:T(2,128)(2,1)S(1)} %bitcast.55, bf16[1,32,64,256]{3,2,1,0:T(8,128)(2,1)S(1)} %copy-done.3, s32[64,256]{1,0:T(8,128)S(1)} %bitcast.60, f32[32,16,1]{0,1,2:T(8,128)S(1)} %get-tuple-element.13, f32[32,16,1]{0,1,2:T(8,128)S(1)} %get-tuple-element.12), kind=kOutput, calls=%fused_computation.7 | convolution fusion | flops 203950080 | bytes 3215360 | tf_op jit(solution)/shard_map/tfc,fscn->tsn/dot_general | solution.py:56
  84.9 0.0 copy-done
  84.9 1.3 fusion.11
  86.2 0.0 all-reduce.2.cloned.1.call-update
  86.2 1.6 copy.29
  87.8 83.3 %all-reduce.2.cloned.1.call-done = bf16[256,256]{1,0:T(8,128)(2,1)} async-done(((bf16[256,256]{1,0:T(8,128)(2,1)}), bf16[256,256]{1,0:T(8,128)(2,1)}) %all-reduce.2.cloned.1.call-update) | async-done | bytes 131088 | tf_op jit(solution)/shard_map/psum | solution.py:72
  171.0 1.3 multiply_bitcast_fusion
  (4 shorter events, 0.1 us)
Async XLA Ops:
  7.2 1.8 copy-start.5
  8.9 4.6 %copy-start.1 = (s32[1,16,1]{1,2,0:T(1,128)S(1)}, s32[1,16,1]{1,2,0:T(1,128)}, u32[]{:S(2)}) copy-start(s32[1,16,1]{1,2,0:T(1,128)} %param.11) | copy-start | bytes 196
  37.7 2.2 %copy-start.2 = (bf16[1,1024,16,128]{3,2,1,0:T(8,128)(2,1)S(1)}, bf16[1,1024,16,128]{3,2,1,0:T(8,128)(2,1)}, u32[]{:S(2)}) copy-start(bf16[1,1024,16,128]{3,2,1,0:T(8,128)(2,1)} %param.10) | copy-start | bytes 12582916
  42.3 40.6 %copy-start.3 = (bf16[1,32,64,256]{3,2,1,0:T(8,128)(2,1)S(1)}, bf16[1,32,64,256]{3,2,1,0:T(8,128)(2,1)}, u32[]{:S(2)}) copy-start(bf16[1,32,64,256]{3,2,1,0:T(8,128)(2,1)} %param.13) | copy-start | bytes 3145732
  42.3 40.6 %copy-start.4 = (s32[1,64,256]{2,1,0:T(8,128)S(1)}, s32[1,64,256]{2,1,0:T(8,128)}, u32[]{:S(2)}) copy-start(s32[1,64,256]{2,1,0:T(8,128)} %param.14) | copy-start | bytes 196612
  44.4 38.5 %all-to-all-start.1 = ((bf16[1,1024,2,256]{3,2,0,1:T(2,128)(2,1)}), bf16[1,1024,2,256]{3,2,0,1:T(2,128)(2,1)S(1)}, u32[]{:S(2)}, u32[]{:S(2)}) async-start(bf16[1,1024,2,256]{3,2,0,1:T(2,128)(2,1)} %copy.26), calls=%async_computation.1 | async-start | bytes 2097152 | tf_op jit(solution)/shard_map/all_to_all | solution.py:54
  54.9 29.9 %copy-start = (f32[1,64]{1,0:T(1,128)S(1)}, f32[1,64]{1,0:T(1,128)}, u32[]{:S(2)}) copy-start(f32[1,64]{1,0:T(1,128)} %param.15) | copy-start | bytes 772
  54.9 116.1 %all-reduce.2.cloned.1.call-start = ((), (), s32[]{:S(2)}) async-start(), calls=%async_computation.2 | async-start | bytes 262144 | tf_op jit(solution)/shard_map/psum | solution.py:72
Sparse Core Ops, SparseCore 0:
  86.3 84.6 all-reduce.1
where the time goes:
time: 180 us; the launch traced here: 179 us
  waiting for transfers between devices  111 us (62%)
  blocking collectives  23.4 us (13%)
  between operations  14.2 us (8%)
  starting transfers between devices  10.6 us (6%)
  matrix products  10.2 us (6%)
  local copies, waits for them, and re-layouts  7.51 us (4%)
  other arithmetic  2.2 us (1%)
    psum x1, waiting for transfers between devices, body(): lax.psum(partial_value.astype(jnp.bfloat16), 'tile').astype(jnp.float32)  83.3 us
    all_to_all x1, waiting for transfers between devices, body(): lax.all_to_all(fields[None], 'freq', split_axis=1, concat_axis=0, tiled=T...  27.8 us
    all_to_all x1, blocking collectives, body(): lax.all_to_all(coeffs, 'tile', split_axis=0, concat_axis=0, tiled=True)  23.4 us
    all_to_all x1, starting transfers between devices, body(): lax.all_to_all(fields[None], 'freq', split_axis=1, concat_axis=0, tiled=T...  10.5 us
    dot_general x1, matrix products, body(): jnp.einsum('irk,rc->ikc', v_factors[0], flat_field, preferred_element_typ...  4.58 us
  transfers between devices with their start and end apart: 2, of which 2 were waited for; matrix products, arithmetic and copies ran while one was open for 1% of the time, Pallas kernels for 0%

commit v1 on v0

--- a/solution.py
+++ b/solution.py
@@ -69,10 +69,12 @@
         flat_focus, flat_weighted, (((0,), (0,)), ((), ())), preferred_element_type=jnp.float32
     )
     normalizer = 1.0 / float(tile_count * trace_length * group_rows)
-    summed_total = lax.psum(partial_value.astype(jnp.bfloat16), "tile").astype(jnp.float32)
+    shares = lax.all_to_all(
+        partial_value.astype(jnp.bfloat16), "tile", split_axis=0, concat_axis=0, tiled=True
+    )
     share_rows = focal_count // tile_count
-    own_rows = lax.dynamic_slice_in_dim(
-        summed_total, lax.axis_index("tile") * share_rows, share_rows, 0
+    own_rows = jnp.sum(
+        shares.reshape(tile_count, share_rows, focal_count).astype(jnp.float32), axis=0
     )
     return (focusing[None], (own_rows * normalizer)[None])
 

time: 180 us -> 90.9 us (0.51)
  waiting for transfers between devices: 111 us -> 33.1 us
  between operations: 14.2 us -> 0.81 us
  starting transfers between devices: 10.6 us -> 14 us
    psum x1 -> x0, waiting for transfers between devices: 83.3 us -> none  [body(): lax.psum(partial_value.astype(jnp.bfloat16), 'tile').astype(jnp.float32)]
    all_to_all x0 -> x1, waiting for transfers between devices: none -> 5.25 us  [body(): lax.all_to_all(partial_value.astype(jnp.bfloat16), 'tile', split_axis=0,...]
    all_to_all x0 -> x1, starting transfers between devices: none -> 3.51 us  [body(): lax.all_to_all(partial_value.astype(jnp.bfloat16), 'tile', split_axis=0,...]
  transfers between devices with their start and end apart: 2 -> 2, of which waited for: 2 -> 2; matrix products, arithmetic and copies ran while one was open for 1% -> 2% of each run, Pallas kernels for 0% -> 0%
where the time goes in v1:
time: 90.9 us; the launch traced here: 90.6 us
  waiting for transfers between devices  33.1 us (36%)
  blocking collectives  23.4 us (26%)
  starting transfers between devices  14 us (15%)
  matrix products  10.2 us (11%)
  local copies, waits for them, and re-layouts  7.47 us (8%)
  other arithmetic  1.53 us (2%)
    all_to_all x1, waiting for transfers between devices, body(): lax.all_to_all(fields[None], 'freq', split_axis=1, concat_axis=0, tiled=T...  27.8 us
    all_to_all x1, blocking collectives, body(): lax.all_to_all(coeffs, 'tile', split_axis=0, concat_axis=0, tiled=True)  23.4 us
    all_to_all x1, starting transfers between devices, body(): lax.all_to_all(fields[None], 'freq', split_axis=1, concat_axis=0, tiled=T...  10.5 us
    all_to_all x1, waiting for transfers between devices, body(): lax.all_to_all(partial_value.astype(jnp.bfloat16), 'tile', split_axis=0,...  5.25 us
    dot_general x1, matrix products, body(): jnp.einsum('irk,rc->ikc', v_factors[0], flat_field, preferred_element_typ...  4.58 us
    unnamed x13, local copies, waits for them, and re-layouts  3.53 us
    all_to_all x1, starting transfers between devices, body(): lax.all_to_all(partial_value.astype(jnp.bfloat16), 'tile', split_axis=0,...  3.51 us
    dot_general x1, matrix products, body(): jnp.dot(u_rows.reshape(tile_rows, -1), stacked_rhs(received), preferred_e...  2.39 us
  transfers between devices with their start and end apart: 2, of which 2 were waited for; matrix products, arithmetic and copies ran while one was open for 2% of the time, Pallas kernels for 0%

profile of v1, /device:TPU:1, one launch (start us, length us, event | category | flops | bytes accessed | tf_op | source)
XLA Modules:
  0.0 90.6 jit_solution(5549969196378328482)
XLA Ops:
  0.6 0.0 copy-start.5
  0.6 1.7 %reshape.192 = bf16[1024,512,1]{1,0,2:T(8,128)(2,1)S(1)} reshape(bf16[1,1024,2,256]{3,2,1,0:T(2,128)(2,1)} %param.8) | data formatting | bytes 2097152 | tf_op jit(solution)/shard_map/reshape;squeeze | solution.py:33
  2.4 0.0 copy-done.5
  2.4 0.0 copy-start.1
  2.4 4.6 %fusion.3 = f32[16,128,512]{2,1,0:T(8,128)S(1)} fusion(bf16[1024,512,1]{1,0,2:T(8,128)(2,1)S(1)} %reshape.192, bf16[1,16,1024,128]{3,2,1,0:T(8,128)(2,1)} %param.9), kind=kOutput, calls=%fused_computation.3 | convolution fusion | flops 2147483648 | bytes 9437184 | tf_op jit(solution)/shard_map/irk,rc->ikc/dot_general | solution.py:34
  7.0 0.0 copy-done.1
  7.0 0.1 fusion.27
  7.1 0.4 fusion.18
  7.5 0.1 pad_maximum_fusion
  7.6 0.1 copy.24
  7.7 23.4 %all_to_all.26 = bf16[16,64,2,256]{3,1,2,0:T(8,128)(2,1)S(1)} all-to-all(bf16[16,64,2,256]{3,1,2,0:T(8,128)(2,1)S(1)} %copy.24), channel_id=1, replica_groups=mesh['freq'=16,'tile'=16] {'tile'}, dimensions={0} | all-to-all | bytes 2097152 | tf_op jit(solution)/shard_map/all_to_all | solution.py:47
  31.1 0.1 slice_bitcast_fusion
  31.2 0.0 copy-start.2
  31.2 0.2 maximum_maximum_fusion
  31.4 1.9 %copy-done.2 = bf16[1,1024,16,128]{3,2,1,0:T(8,128)(2,1)S(1)} copy-done((bf16[1,1024,16,128]{3,2,1,0:T(8,128)(2,1)S(1)}, bf16[1,1024,16,128]{3,2,1,0:T(8,128)(2,1)}, u32[]{:S(2)}) %copy-start.2) | copy-done | bytes 4194328
  33.4 2.4 %fusion.7 = bf16[512,1024]{1,0:T(8,128)(2,1)S(1)} fusion(bf16[2048,512]{1,0:T(8,128)(2,1)S(1)} %bitcast.55, bf16[128,8,16,128]{3,2,1,0:T(8,128)(2,1)S(1)} %bitcast.60), kind=kOutput, calls=%fused_computation.12 | convolution fusion | flops 2148007936 | bytes 7340032 | tf_op jit(solution)/shard_map/dot_general | solution.py:49
  35.8 0.0 copy-start.3
  35.8 0.0 copy-start.4
  35.8 2.0 %copy.26 = bf16[1,1024,2,256]{3,2,0,1:T(2,128)(2,1)} copy(bf16[1,1024,2,256]{1,3,2,0:T(8,128)(2,1)S(1)} %bitcast.57) | data formatting | bytes 2097152 | tf_op jit(solution)/shard_map/convert_element_type | solution.py:52
  37.8 10.5 %all-to-all-start.1 = ((bf16[1,1024,2,256]{3,2,0,1:T(2,128)(2,1)}), bf16[1,1024,2,256]{3,2,0,1:T(2,128)(2,1)S(1)}, u32[]{:S(2)}, u32[]{:S(2)}) async-start(bf16[1,1024,2,256]{3,2,0,1:T(2,128)(2,1)} %copy.26), calls=%async_computation.1 | async-start | bytes 2097152 | tf_op jit(solution)/shard_map/all_to_all | solution.py:54
  48.4 0.0 copy-start
  48.4 0.1 multiply_cosine_fusion
  48.5 27.8 %all-to-all-done.1 = bf16[1,1024,2,256]{3,2,0,1:T(2,128)(2,1)S(1)} async-done(((bf16[1,1024,2,256]{3,2,0,1:T(2,128)(2,1)}), bf16[1,1024,2,256]{3,2,0,1:T(2,128)(2,1)S(1)}, u32[]{:S(2)}, u32[]{:S(2)}) %all-to-all-start.1) | async-done | bytes 1048608 | tf_op jit(solution)/shard_map/all_to_all | solution.py:54
  76.3 0.0 copy-done.3
  76.4 0.0 copy-done.4
  76.4 1.9 %fusion.5 = bf16[32,64,256]{2,0,1:T(8,128)(2,1)S(1)} fusion(bf16[16,64,2,256]{3,2,1,0:T(2,128)(2,1)S(1)} %bitcast.56, bf16[1,32,64,256]{3,2,1,0:T(8,128)(2,1)S(1)} %copy-done.3, s32[64,256]{1,0:T(8,128)S(1)} %bitcast.61, f32[32,16,1]{0,1,2:T(8,128)S(1)} %get-tuple-element.13, f32[32,16,1]{0,1,2:T(8,128)S(1)} %get-tuple-element.12), kind=kOutput, calls=%fused_computation.7 | convolution fusion | flops 203950080 | bytes 3215360 | tf_op jit(solution)/shard_map/tfc,fscn->tsn/dot_general | solution.py:56
  78.3 0.0 copy-done
  78.3 1.3 %fusion.11 = bf16[256,256]{1,0:T(8,128)(2,1)} fusion(bf16[32,64,256]{2,0,1:T(8,128)(2,1)S(1)} %fusion.5, f32[64]{0:T(128)S(1)} %bitcast.58), kind=kOutput, calls=%fused_computation.14 | convolution fusion | flops 270073856 | bytes 1179904 | tf_op jit(solution)/shard_map/dot_general | solution.py:68
  79.6 3.5 %all-to-all-start.2 = ((bf16[16,16,256]{2,1,0:T(8,128)(2,1)}), bf16[16,16,256]{2,1,0:T(8,128)(2,1)S(1)}, u32[]{:S(2)}, u32[]{:S(2)}) async-start(bf16[16,16,256]{2,1,0:T(8,128)(2,1)} %bitcast.19), calls=%async_computation.2 | async-start | bytes 262144 | tf_op jit(solution)/shard_map/all_to_all | solution.py:72
  83.1 1.6 %copy.29 = bf16[1,32,64,256]{3,2,1,0:T(8,128)(2,1)} copy(bf16[1,32,64,256]{3,1,2,0:T(8,128)(2,1)S(1)} %bitcast.54) | data formatting | bytes 2097152
  84.7 5.2 %all-to-all-done.2 = bf16[16,16,256]{2,1,0:T(8,128)(2,1)S(1)} async-done(((bf16[16,16,256]{2,1,0:T(8,128)(2,1)}), bf16[16,16,256]{2,1,0:T(8,128)(2,1)S(1)}, u32[]{:S(2)}, u32[]{:S(2)}) %all-to-all-start.2) | async-done | bytes 131104 | tf_op jit(solution)/shard_map/all_to_all | solution.py:72
  89.9 0.6 multiply_bitcast_fusion
  (5 shorter events, 0.1 us)
Async XLA Ops:
  0.6 1.8 %copy-start.5 = (s32[1,16,1]{1,2,0:T(1,128)S(1)}, s32[1,16,1]{1,2,0:T(1,128)}, u32[]{:S(2)}) copy-start(s32[1,16,1]{1,2,0:T(1,128)} %param.12) | copy-start | bytes 196
  2.4 4.6 %copy-start.1 = (s32[1,16,1]{1,2,0:T(1,128)S(1)}, s32[1,16,1]{1,2,0:T(1,128)}, u32[]{:S(2)}) copy-start(s32[1,16,1]{1,2,0:T(1,128)} %param.11) | copy-start | bytes 196
  31.2 2.2 %copy-start.2 = (bf16[1,1024,16,128]{3,2,1,0:T(8,128)(2,1)S(1)}, bf16[1,1024,16,128]{3,2,1,0:T(8,128)(2,1)}, u32[]{:S(2)}) copy-start(bf16[1,1024,16,128]{3,2,1,0:T(8,128)(2,1)} %param.10) | copy-start | bytes 12582916
  35.8 40.6 %copy-start.3 = (bf16[1,32,64,256]{3,2,1,0:T(8,128)(2,1)S(1)}, bf16[1,32,64,256]{3,2,1,0:T(8,128)(2,1)}, u32[]{:S(2)}) copy-start(bf16[1,32,64,256]{3,2,1,0:T(8,128)(2,1)} %param.13) | copy-start | bytes 3145732
  35.8 40.6 %copy-start.4 = (s32[1,64,256]{2,1,0:T(8,128)S(1)}, s32[1,64,256]{2,1,0:T(8,128)}, u32[]{:S(2)}) copy-start(s32[1,64,256]{2,1,0:T(8,128)} %param.14) | copy-start | bytes 196612
  37.8 38.5 %all-to-all-start.1 = ((bf16[1,1024,2,256]{3,2,0,1:T(2,128)(2,1)}), bf16[1,1024,2,256]{3,2,0,1:T(2,128)(2,1)S(1)}, u32[]{:S(2)}, u32[]{:S(2)}) async-start(bf16[1,1024,2,256]{3,2,0,1:T(2,128)(2,1)} %copy.26), calls=%async_computation.1 | async-start | bytes 2097152 | tf_op jit(solution)/shard_map/all_to_all | solution.py:54
  48.4 29.9 %copy-start = (f32[1,64]{1,0:T(1,128)S(1)}, f32[1,64]{1,0:T(1,128)}, u32[]{:S(2)}) copy-start(f32[1,64]{1,0:T(1,128)} %param.15) | copy-start | bytes 772
  79.6 10.3 %all-to-all-start.2 = ((bf16[16,16,256]{2,1,0:T(8,128)(2,1)}), bf16[16,16,256]{2,1,0:T(8,128)(2,1)S(1)}, u32[]{:S(2)}, u32[]{:S(2)}) async-start(bf16[16,16,256]{2,1,0:T(8,128)(2,1)} %bitcast.19), calls=%async_computation.2 | async-start | bytes 262144 | tf_op jit(solution)/shard_map/all_to_all | solution.py:72

commit v2 on v1

v2 whole, which is shorter than its diff:
```python
import functools
import math

import jax
import jax.numpy as jnp
from jax import lax
from jax.experimental import pallas as pl
from jax.experimental.pallas import tpu as pltpu
from jax.sharding import PartitionSpec as P


LANES = 128
ORDER = ((1, 7), (2, 6), (3, 5), (4, 0))


def spec(block=None, index=None):
    if block is None:
        return pl.BlockSpec(memory_space=pltpu.VMEM)
    return pl.BlockSpec(block, index)


def moments_kernel(ranks, mask, field_hbm, v_hbm, out, field, v_all, field_t, sems):
    rows, _, focal = field.shape
    tiles, _, wide = v_all.shape
    groups = sems.shape[0] - 1
    group = tiles // groups
    fetch = pltpu.make_async_copy(field_hbm, field, sems.at[groups])
    fetch.start()
    fetches = [
        pltpu.make_async_copy(
            v_hbm.at[pl.ds(s * group, group)], v_all.at[pl.ds(s * group, group)], sems.at[s]
        )
        for s in range(groups)
    ]
    for copy in fetches:
        copy.start()
    source = lax.broadcasted_iota(jnp.int32, (2 * LANES, 2 * LANES), 0)
    target = lax.broadcasted_iota(jnp.int32, (2 * LANES, 2 * LANES), 1)
    wanted = 2 * lax.rem(target, LANES) + lax.div(target, LANES)
    apart = (source == wanted).astype(jnp.float32).astype(jnp.bfloat16)
    lane = lax.broadcasted_iota(jnp.int32, (focal, wide), 1)
    sign = jnp.where(lane < wide // 2, -1.0, 1.0)
    level = lax.rem(lane, wide // 2)
    fetch.wait()
    for b in range(rows // LANES):
        for q in range(focal // LANES):
            block = field[b * LANES : (b + 1) * LANES, :, q * LANES : (q + 1) * LANES]
            turned = lax.dot_general(
                block.reshape(2 * LANES, LANES),
                apart,
                (((0,), (0,)), ((), ())),
                preferred_element_type=jnp.float32,
            ).astype(jnp.bfloat16)
            at = slice(b * LANES, (b + 1) * LANES)
            field_t[q * LANES : (q + 1) * LANES, at] = turned[:, :LANES]
            field_t[focal + q * LANES : focal + (q + 1) * LANES, at] = turned[:, LANES:]
    for s in range(groups):
        fetches[s].wait()
        both = jnp.concatenate([v_all[s * group + n] for n in range(group)], axis=1)
        products = jnp.dot(field_t[...], both, preferred_element_type=jnp.float32)
        for n in range(group):
            i = s * group + n
            a = products[:focal, n * wide : (n + 1) * wide]
            b = products[focal:, n * wide : (n + 1) * wide]
            moments = a + sign * pltpu.roll(b, wide // 2, 1)
            kept = jnp.where(mask[i] > 0, ranks[i], 0)
            out[i] = jnp.where(level < kept, moments, 0.0).astype(jnp.bfloat16)


def moments(ranks, mask, field, v_tiles, groups=2):
    tiles, rows, wide = v_tiles.shape
    focal = field.shape[2]
    return pl.pallas_call(
        moments_kernel,
        in_specs=[
            pl.BlockSpec(memory_space=pltpu.SMEM),
            pl.BlockSpec(memory_space=pltpu.SMEM),
            pl.BlockSpec(memory_space=pltpu.HBM),
            pl.BlockSpec(memory_space=pltpu.HBM),
        ],
        out_specs=spec(),
        scratch_shapes=[
            pltpu.VMEM(field.shape, jnp.bfloat16),
            pltpu.VMEM(v_tiles.shape, jnp.bfloat16),
            pltpu.VMEM((2 * focal, rows), jnp.bfloat16),
            pltpu.SemaphoreType.DMA((groups + 1,)),
        ],
        out_shape=jax.ShapeDtypeStruct((tiles, focal, wide), jnp.bfloat16),
        cost_estimate=pl.CostEstimate(
            flops=4 * tiles * rows * wide * focal, bytes_accessed=6 << 20, transcendentals=0
        ),
        compiler_params=pltpu.CompilerParams(vmem_limit_bytes=60 << 20),
        name="moments",
    )(ranks, mask, field, v_tiles)


def flatten_kernel(place, u_tiles, u_rows):
    rows = u_tiles.shape[0]
    u_rows[...] = u_tiles[...].reshape(rows, -1)


def flatten(place, u_tiles, distances, chips):
    rows, tiles, wide = u_tiles.shape
    block = rows // chips

    def source(s, where):
        ahead = sum((jnp.where(s == n, d, 0) for n, d in enumerate(distances)), 0)
        return (lax.rem(where[0] + ahead, chips), 0, 0)

    return pl.pallas_call(
        flatten_kernel,
        grid_spec=pltpu.PrefetchScalarGridSpec(
            num_scalar_prefetch=1,
            grid=(len(distances),),
            in_specs=[spec((block, tiles, wide), source)],
            out_specs=spec((block, tiles * wide), lambda s, where: (s, 0)),
        ),
        out_shape=jax.ShapeDtypeStruct((len(distances) * block, tiles * wide), jnp.bfloat16),
        cost_estimate=pl.CostEstimate(flops=1 << 22, bytes_accessed=8 << 20, transcendentals=0),
        compiler_params=pltpu.CompilerParams(vmem_limit_bytes=60 << 20),
    )(place, u_tiles)


def terms_kernel(received, terms):
    tiles, focal, wide = received.shape
    lane = lax.broadcasted_iota(jnp.int32, (focal, wide), 1)
    sign = jnp.where(lane < wide // 2, 1.0, -1.0)
    for j in range(tiles):
        coeffs = received[j].astype(jnp.float32)
        at = slice(j * wide, (j + 1) * wide)
        terms[:focal, at] = (coeffs * sign).astype(jnp.bfloat16)
        terms[focal:, at] = pltpu.roll(coeffs, wide // 2, 1).astype(jnp.bfloat16)


def rank_terms(received):
    tiles, focal, wide = received.shape
    return pl.pallas_call(
        terms_kernel,
        in_specs=[spec()],
        out_specs=spec(),
        out_shape=jax.ShapeDtypeStruct((2 * focal, tiles * wide), jnp.bfloat16),
        cost_estimate=pl.CostEstimate(flops=1 << 22, bytes_accessed=3 << 20, transcendentals=0),
        compiler_params=pltpu.CompilerParams(vmem_limit_bytes=8 << 20),
        name="terms",
    )(received)


def fields_kernel(place, terms, u_rows, *outs):
    sub = outs[0].shape[1]
    core = place[1]
    product = lax.dot_general(
        u_rows[...], terms[...], (((1,), (1,)), ((), ())), preferred_element_type=jnp.float32
    ).astype(jnp.bfloat16)
    for n, out in enumerate(outs):
        base = 2 * sub * n
        out[core] = product[base : base + sub]
        out[1 - core] = product[base + sub : base + 2 * sub]


def fields(place, terms, u_rows, distances):
    rows, depth = u_rows.shape
    wide = terms.shape[0]
    sub = rows // (2 * len(distances))
    return pl.pallas_call(
        fields_kernel,
        in_specs=[pl.BlockSpec(memory_space=pltpu.SMEM), spec(), spec()],
        out_specs=[spec()] * len(distances),
        out_shape=[jax.ShapeDtypeStruct((2, sub, wide), jnp.bfloat16)] * len(distances),
        cost_estimate=pl.CostEstimate(
            flops=2 * rows * depth * wide, bytes_accessed=3 << 20, transcendentals=0
        ),
        compiler_params=pltpu.CompilerParams(vmem_limit_bytes=14 << 20),
    )(place, terms, u_rows)


def halves(terms, kind, period):
    if not terms:
        return None
    half = period // 2
    if len(terms) == 1 or half % 2:
        return direct(terms, kind, period, half + 1)
    even = {n // 2: v for n, v in terms.items() if n % 2 == 0}
    odd = {n: v for n, v in terms.items() if n % 2}
    quarter = half // 2
    a = halves(even, kind, half) if even else [None] * (quarter + 1)
    b = direct(odd, kind, period, quarter + 1)
    out = [None] * (half + 1)
    for t in range(quarter + 1):
        out[t] = plus(a[t], b[t])
        if kind == "cos":
            out[half - t] = plus(a[t], minus(b[t]))
        else:
            out[half - t] = plus(minus(a[t]), b[t])
    return out


def minus(value):
    return None if value is None else ("-", value)


def plus(a, b):
    if a is None or b is None:
        a = b if a is None else a
        if isinstance(a, tuple):
            return -a[1]
        return a
    if isinstance(b, tuple):
        return a - b[1]
    if isinstance(a, tuple):
        return b - a[1]
    return a + b


def direct(terms, kind, period, count):
    out = []
    for t in range(count):
        total = None
        for n, value in terms.items():
            turn = (n * t) % period
            angle = 2.0 * math.pi * turn / period
            weight = math.cos(angle) if kind == "cos" else math.sin(angle)
            if abs(weight) < 1e-9:
                continue
            if abs(weight - 1.0) < 1e-9:
                total = plus(total, value)
            elif abs(weight + 1.0) < 1e-9:
                total = plus(total, minus(value)) if total is not None else -value
            else:
                total = plus(total, value * jnp.float32(weight))
        out.append(total)
    return out


def series_kernel(place, *refs, chips, steps):
    own, swapped = refs[:chips], refs[chips : 2 * chips]
    initial, mutes, taper, focusing, partial, spectra, signal, weighted, total = refs[2 * chips :]
    step = pl.program_id(0)
    chip, core = place[0], place[1]
    trace, rows, focal = initial.shape
    freqs = 2 * chips
    scale = 1.0 / math.sqrt(freqs)
    for d in range(chips):
        source = 2 * lax.rem(chip + chips - d, chips)
        for value, f in ((own[d][...], source + core), (swapped[d][...], source + 1 - core)):
            value = value.astype(jnp.float32) * scale
            spectra[f, 0] = value[:, :focal]
            spectra[f, 1] = value[:, focal:]
    for r in range(rows // 8):
        for q in range(focal // LANES):
            at = (slice(r * 8, (r + 1) * 8), slice(q * LANES, (q + 1) * LANES))
            cosines = halves({f + 1: spectra[(f, 0) + at] for f in range(freqs)}, "cos", trace)
            sines = halves({f + 1: spectra[(f, 1) + at] for f in range(freqs)}, "sin", trace)
            for t in range(trace // 2 + 1):
                signal[(t,) + at] = plus(cosines[t], minus(sines[t]))
                if 0 < t < trace // 2:
                    signal[(trace - t,) + at] = plus(cosines[t], sines[t])
    start = mutes[...]
    weight = taper[...]
    for t in range(trace):
        silenced = jnp.where(t < start, signal[t], 0.0)
        after = (initial[t].astype(jnp.float32) - silenced).astype(jnp.bfloat16)
        focusing[t] = after
        weighted[t] = (after.astype(jnp.float32) * weight).astype(jnp.bfloat16)
    product = lax.dot_general(
        focusing[...].reshape(trace * rows, focal),
        weighted[...].reshape(trace * rows, focal),
        (((0,), (0,)), ((), ())),
        preferred_element_type=jnp.float32,
    )

    @pl.when(step == 0)
    def _():
        total[...] = product

    @pl.when(step > 0)
    def _():
        total[...] += product

    @pl.when(step == steps - 1)
    def _():
        partial[...] = total[...].astype(jnp.bfloat16)


def series_update(place, own, swapped, initial, mutes, taper, rows=16):
    chips = len(own)
    _, trace, sub, focal = initial.shape
    steps = sub // rows
    times = spec((None, trace, rows, focal), lambda s: (0, 0, s, 0))
    return pl.pallas_call(
        functools.partial(series_kernel, chips=chips, steps=steps),
        grid=(steps,),
        in_specs=[pl.BlockSpec(memory_space=pltpu.SMEM)]
        + [spec((None, rows, 2 * focal), lambda s: (0, s, 0))] * chips
        + [spec((rows, 2 * focal), lambda s: (s, 0))] * chips
        + [
            times,
            spec((None, rows, focal), lambda s: (0, s, 0)),
            spec((rows, 1), lambda s: (s, 0)),
        ],
        out_specs=[times, spec((focal, focal), lambda s: (0, 0))],
        scratch_shapes=[
            pltpu.VMEM((2 * chips, 2, rows, focal), jnp.float32),
            pltpu.VMEM((trace, rows, focal), jnp.float32),
            pltpu.VMEM((trace, rows, focal), jnp.bfloat16),
            pltpu.VMEM((focal, focal), jnp.float32),
        ],
        out_shape=[
            jax.ShapeDtypeStruct(initial.shape, jnp.bfloat16),
            jax.ShapeDtypeStruct((focal, focal), jnp.bfloat16),
        ],
        cost_estimate=pl.CostEstimate(
            flops=2 * trace * sub * focal * focal, bytes_accessed=4 << 20, transcendentals=0
        ),
        compiler_params=pltpu.CompilerParams(vmem_limit_bytes=14 << 20),
        name="series",
    )(place, *own, *swapped, initial, mutes, taper)


def swap_cores(values, freq_count):
    return lax.ppermute(values, "freq", [(f, f ^ 1) for f in range(freq_count)])


def shift_chips(values, distance, freq_count):
    pairs = [(f, (f + 2 * distance) % freq_count) for f in range(freq_count)]
    return lax.ppermute(values, "freq", pairs)


def update(focal_field, v_factors, u_factors, ranks, tile_mask, initial_focus, mute_starts, taper):
    tile_count = lax.axis_size("tile")
    freq_count = lax.axis_size("freq")
    me = lax.axis_index("freq")
    chips = freq_count // 2
    place = jnp.stack([me // 2, lax.rem(me, 2)])
    _, _, focal_count = focal_field.shape[1:]
    u_rows = [flatten(place, u_factors[0], distances, chips) for distances in ORDER]
    coeffs = moments(ranks[0, :, 0], tile_mask[0, :, 0], focal_field[0], v_factors[0])
    received = lax.all_to_all(coeffs, "tile", split_axis=0, concat_axis=0, tiled=True)
    terms = rank_terms(received)
    own, swapped = [None] * chips, [None] * chips
    for n, distances in enumerate(ORDER):
        blocks = fields(place, terms, u_rows[n], distances)
        for d, block in zip(distances, blocks):
            own[d] = shift_chips(block, d, freq_count) if d else block
            swapped[d] = swap_cores(own[d][1], freq_count)
    focusing, partial = series_update(
        place, own, swapped, initial_focus, mute_starts, taper[0][:, None]
    )
    shares = lax.all_to_all(partial, "tile", split_axis=0, concat_axis=0, tiled=True)
    trace_length, group_rows = initial_focus.shape[1:3]
    normalizer = 1.0 / float(tile_count * trace_length * group_rows)
    share_rows = focal_count // tile_count
    own_rows = jnp.sum(
        shares.reshape(tile_count, share_rows, focal_count).astype(jnp.float32), axis=0
    )
    return (focusing, (own_rows * normalizer)[None])


def solution(mesh):
    placed = (
        P("freq", "tile", None, None),
        P("freq", None, "tile", None),
        P("freq", "tile", None, None),
        P("freq", None, "tile"),
        P("freq", None, "tile"),
        P("tile", None, "freq", None),
        P("tile", "freq", None),
        P("tile", "freq"),
    )
    return jax.shard_map(
        update,
        mesh=mesh,
        in_specs=placed,
        out_specs=(P("tile", None, "freq", None), P("freq", "tile", None)),
        check_vma=False,
    )
```

time: 90.9 us -> 91.9 us (1.011); the launches traced: 90.6 us -> 90.6 us
  starting transfers between devices: 14 us -> 43.6 us
  Pallas kernels: 0 us -> 27.6 us
  waiting for transfers between devices: 33.1 us -> 5.87 us
  blocking collectives: 23.4 us -> 10 us
  matrix products: 10.2 us -> 0 us
  local copies, waits for them, and re-layouts: 7.47 us -> 1.39 us
    ppermute x0 -> x15, starting transfers between devices: none -> 36 us  [the longest x8 19.2 us: swap_cores(): return lax.ppermute(values, 'freq', [(f, f ^ 1) for f in range(freq_count)])]
    all_to_all x2 -> x1, waiting for transfers between devices: 33.1 us -> 3.97 us  [update(): lax.all_to_all(coeffs, 'tile', split_axis=0, concat_axis=0, tiled=True)]
    pallas_call x0 -> x11, Pallas kernels: none -> 27.6 us  [the longest x4 11.4 us: flatten(): pl.pallas_call(flatten_kernel, grid_spec=pltpu.PrefetchScalarGridSpec(num...]
    all_to_all x1, blocking collectives: 23.4 us -> 10 us  [update(): lax.all_to_all(partial, 'tile', split_axis=0, concat_axis=0, tiled=True)]
    dot_general x4 -> x0, matrix products: 10.2 us -> none  [the longest x1 4.58 us: body(): jnp.einsum('irk,rc->ikc', v_factors[0], flat_field, preferred_element_typ...]
    all_to_all x2 -> x1, starting transfers between devices: 14 us -> 7.58 us  [update(): lax.all_to_all(coeffs, 'tile', split_axis=0, concat_axis=0, tiled=True)]
    unnamed x13 -> x16, local copies, waits for them, and re-layouts: 3.53 us -> 1.25 us
    convert_element_type x1 -> x0, local copies, waits for them, and re-layouts: 2.04 us -> none  [body(): fields = product.reshape(tile_rows, 2, columns).astype(jnp.bfloat16)]
  transfers between devices with their start and end apart: 2 -> 16, of which waited for: 2 -> 7; matrix products, arithmetic and copies ran while one was open for 2% -> 1% of each run, Pallas kernels for 0% -> 15%
where the time goes in v2:
time: 91.9 us; the launch traced here: 90.6 us
  starting transfers between devices  43.6 us (47%)
  Pallas kernels  27.6 us (30%)
  blocking collectives  10 us (11%)
  waiting for transfers between devices  5.87 us (6%)
  local copies, waits for them, and re-layouts  1.39 us (2%)
  other arithmetic  1.28 us (1%)
    ppermute x8, starting transfers between devices, swap_cores(): return lax.ppermute(values, 'freq', [(f, f ^ 1) for f in range(freq_count)])  19.2 us
    ppermute x7, starting transfers between devices, shift_chips(): return lax.ppermute(values, 'freq', pairs)  16.8 us
    pallas_call x4, Pallas kernels, flatten(): pl.pallas_call(flatten_kernel, grid_spec=pltpu.PrefetchScalarGridSpec(num...  11.4 us
    all_to_all x1, blocking collectives, update(): lax.all_to_all(partial, 'tile', split_axis=0, concat_axis=0, tiled=True)  10 us
    all_to_all x1, starting transfers between devices, update(): lax.all_to_all(coeffs, 'tile', split_axis=0, concat_axis=0, tiled=True)  7.58 us
    pallas_call x1, Pallas kernels, moments(): pl.pallas_call(moments_kernel, in_specs=[pl.BlockSpec(memory_space=pltpu....  6.48 us
    pallas_call x4, Pallas kernels, fields(): pl.pallas_call(fields_kernel, in_specs=[pl.BlockSpec(memory_space=pltpu.S...  5.12 us
    pallas_call x1, Pallas kernels, series_update(): pl.pallas_call(functools.partial(series_kernel, chips=chips, steps=steps)...  4.16 us
  transfers between devices with their start and end apart: 16, of which 7 were waited for; matrix products, arithmetic and copies ran while one was open for 1% of the time, Pallas kernels for 15%

profile of v2, /device:TPU:1, one launch (start us, length us, event | category | flops | bytes accessed | tf_op | source)
XLA Modules:
  0.0 90.6 jit_solution(15535900485835805920)
XLA Ops:
  0.6 6.5 %moments.1 = bf16[16,256,128]{2,1,0:T(8,128)(2,1)} custom-call(s32[16]{0:T(128)} %bitcast.35, s32[16]{0:T(128)} %bitcast.36, bf16[1024,2,256]{2,1,0:T(2,128)(2,1)} %bitcast.34, bf16[16,1024,128]{2,1,0:T(8,128)(2,1)} %bitcast.33), custom_call_target="tpu_custom_call" | custom-call | flops 2147483648 | bytes 6291456 | tf_op jit(solution)/shard_map/moments/pallas_call | solution.py:73
  7.1 7.6 %all-to-all-start = ((bf16[16,256,128]{2,1,0:T(8,128)(2,1)}), bf16[16,256,128]{2,1,0:T(8,128)(2,1)S(1)}, u32[]{:S(2)}, u32[]{:S(2)}) async-start(bf16[16,256,128]{2,1,0:T(8,128)(2,1)} %moments.1), calls=%async_computation | async-start | bytes 2097152 | tf_op jit(solution)/shard_map/all_to_all | solution.py:337
  14.7 0.7 pad_add_fusion.place
  15.4 2.8 %shard_map.95.u_rows = bf16[256,2048]{1,0:T(8,128)(2,1)} custom-call(s32[2]{0:T(128)} %pad_add_fusion.place, bf16[1024,16,128]{2,1,0:T(8,128)(2,1)} %bitcast.28), custom_call_target="tpu_custom_call" | custom-call | flops 4194304 | bytes 8388608 | tf_op jit(solution)/shard_map/pallas_call | solution.py:110
  18.2 2.8 %shard_map.97.u_rows = bf16[256,2048]{1,0:T(8,128)(2,1)} custom-call(s32[2]{0:T(128)} %pad_add_fusion.place, bf16[1024,16,128]{2,1,0:T(8,128)(2,1)} %bitcast.29), custom_call_target="tpu_custom_call" | custom-call | flops 4194304 | bytes 8388608 | tf_op jit(solution)/shard_map/pallas_call | solution.py:110
  21.0 2.8 %shard_map.99.u_rows = bf16[256,2048]{1,0:T(8,128)(2,1)} custom-call(s32[2]{0:T(128)} %pad_add_fusion.place, bf16[1024,16,128]{2,1,0:T(8,128)(2,1)} %bitcast.30), custom_call_target="tpu_custom_call" | custom-call | flops 4194304 | bytes 8388608 | tf_op jit(solution)/shard_map/pallas_call | solution.py:110
  23.8 0.0 copy-start.6
  23.8 2.9 %shard_map.101.u_rows = bf16[256,2048]{1,0:T(8,128)(2,1)} custom-call(s32[2]{0:T(128)} %pad_add_fusion.place, bf16[1024,16,128]{2,1,0:T(8,128)(2,1)} %bitcast.31), custom_call_target="tpu_custom_call" | custom-call | flops 4194304 | bytes 8388608 | tf_op jit(solution)/shard_map/pallas_call | solution.py:110
  26.8 0.0 copy-start.2
  26.8 0.0 copy-start.1
  26.8 4.0 %all-to-all-done.received = bf16[16,256,128]{2,1,0:T(8,128)(2,1)S(1)} async-done(((bf16[16,256,128]{2,1,0:T(8,128)(2,1)}), bf16[16,256,128]{2,1,0:T(8,128)(2,1)S(1)}, u32[]{:S(2)}, u32[]{:S(2)}) %all-to-all-start) | async-done | bytes 1048608 | tf_op jit(solution)/shard_map/all_to_all | solution.py:337
  30.7 0.4 terms.1
  31.2 0.0 copy-done.6
  31.2 0.0 copy-start.3
  31.2 1.2 %copy-done.3 = bf16[256,2048]{1,0:T(8,128)(2,1)S(1)} copy-done((bf16[256,2048]{1,0:T(8,128)(2,1)S(1)}, bf16[256,2048]{1,0:T(8,128)(2,1)}, u32[]{:S(2)}) %copy-start.3) | copy-done | bytes 1048600
  32.4 0.0 copy-start
  32.4 1.3 %shard_map.96 = (bf16[2,64,512]{2,1,0:T(8,128)(2,1)S(1)}, bf16[2,64,512]{2,1,0:T(8,128)(2,1)S(1)}) custom-call(s32[2]{0:T(128)S(1)} %copy-done.6, bf16[512,2048]{1,0:T(8,128)(2,1)S(1)} %terms.1, bf16[256,2048]{1,0:T(8,128)(2,1)S(1)} %copy-done.3), custom_call_target="tpu_custom_call" | custom-call | flops 536870912 | bytes 3145728 | tf_op jit(solution)/shard_map/pallas_call | solution.py:164
  33.7 0.0 copy-done.2
  33.7 1.3 %shard_map.98 = (bf16[2,64,512]{2,1,0:T(8,128)(2,1)S(1)}, bf16[2,64,512]{2,1,0:T(8,128)(2,1)S(1)}) custom-call(s32[2]{0:T(128)S(1)} %copy-done.6, bf16[512,2048]{1,0:T(8,128)(2,1)S(1)} %terms.1, bf16[256,2048]{1,0:T(8,128)(2,1)S(1)} %copy-done.2), custom_call_target="tpu_custom_call" | custom-call | flops 536870912 | bytes 3145728 | tf_op jit(solution)/shard_map/pallas_call | solution.py:164
  35.0 0.0 copy-start.7
  35.0 0.0 copy-start.4
  35.0 0.0 copy-start.5
  35.1 1.7 %collective-permute-start = (bf16[2,64,512]{2,1,0:T(8,128)(2,1)S(1)}, bf16[2,64,512]{2,1,0:T(8,128)(2,1)S(1)}, u32[]{:S(2)}, u32[]{:S(2)}) collective-permute-start(bf16[2,64,512]{2,1,0:T(8,128)(2,1)S(1)} %get-tuple-element.13), channel_id=1, source_target_pairs={{0,32},{16,48},{32,64},{48,80},{64,96},{80,112},{96,128},{112,144}... | collective-permute-start | bytes 393224 | tf_op jit(solution)/shard_map/ppermute | solution.py:325
  36.8 0.0 copy-done.1
  36.8 1.3 %shard_map.100 = (bf16[2,64,512]{2,1,0:T(8,128)(2,1)S(1)}, bf16[2,64,512]{2,1,0:T(8,128)(2,1)S(1)}) custom-call(s32[2]{0:T(128)S(1)} %copy-done.6, bf16[512,2048]{1,0:T(8,128)(2,1)S(1)} %terms.1, bf16[256,2048]{1,0:T(8,128)(2,1)S(1)} %copy-done.1), custom_call_target="tpu_custom_call" | custom-call | flops 536870912 | bytes 3145728 | tf_op jit(solution)/shard_map/pallas_call | solution.py:164
  38.1 3.1 %collective-permute-start.1 = (bf16[2,64,512]{2,1,0:T(8,128)(2,1)S(1)}, bf16[2,64,512]{2,1,0:T(8,128)(2,1)S(1)}, u32[]{:S(2)}, u32[]{:S(2)}) collective-permute-start(bf16[2,64,512]{2,1,0:T(8,128)(2,1)S(1)} %get-tuple-element.14), channel_id=1, source_target_pairs={{0,64},{16,80},{32,96},{48,112},{64,128},{80,144},{96,160},{112,17... | collective-permute-start | bytes 393224 | tf_op jit(solution)/shard_map/ppermute | solution.py:325
  41.1 0.0 copy-done
  41.1 1.3 %shard_map.102 = (bf16[2,64,512]{2,1,0:T(8,128)(2,1)S(1)}, bf16[2,64,512]{2,1,0:T(8,128)(2,1)S(1)}) custom-call(s32[2]{0:T(128)S(1)} %copy-done.6, bf16[512,2048]{1,0:T(8,128)(2,1)S(1)} %terms.1, bf16[256,2048]{1,0:T(8,128)(2,1)S(1)} %copy-done), custom_call_target="tpu_custom_call" | custom-call | flops 536870912 | bytes 3145728 | tf_op jit(solution)/shard_map/pallas_call | solution.py:164
  42.4 3.8 %collective-permute-start.2 = (bf16[2,64,512]{2,1,0:T(8,128)(2,1)S(1)}, bf16[2,64,512]{2,1,0:T(8,128)(2,1)S(1)}, u32[]{:S(2)}, u32[]{:S(2)}) collective-permute-start(bf16[2,64,512]{2,1,0:T(8,128)(2,1)S(1)} %get-tuple-element.15), channel_id=1, source_target_pairs={{0,96},{16,112},{32,128},{48,144},{64,160},{80,176},{96,192},{112,... | collective-permute-start | bytes 393224 | tf_op jit(solution)/shard_map/ppermute | solution.py:325
  46.3 0.6 collective-permute-start.3
  46.8 4.4 %collective-permute-start.4 = (bf16[2,64,512]{2,1,0:T(8,128)(2,1)S(1)}, bf16[2,64,512]{2,1,0:T(8,128)(2,1)S(1)}, u32[]{:S(2)}, u32[]{:S(2)}) collective-permute-start(bf16[2,64,512]{2,1,0:T(8,128)(2,1)S(1)} %get-tuple-element.17), channel_id=1, source_target_pairs={{0,160},{16,176},{32,192},{48,208},{64,224},{80,240},{96,0},{112,1... | collective-permute-start | bytes 393224 | tf_op jit(solution)/shard_map/ppermute | solution.py:325
  51.2 0.0 collective-permute-done.refs_1_
  51.2 2.5 %collective-permute-start.5 = (bf16[2,64,512]{2,1,0:T(8,128)(2,1)S(1)}, bf16[2,64,512]{2,1,0:T(8,128)(2,1)S(1)}, u32[]{:S(2)}, u32[]{:S(2)}) collective-permute-start(bf16[2,64,512]{2,1,0:T(8,128)(2,1)S(1)} %get-tuple-element.18), channel_id=1, source_target_pairs={{0,192},{16,208},{32,224},{48,240},{64,0},{80,16},{96,32},{112,48}... | collective-permute-start | bytes 393224 | tf_op jit(solution)/shard_map/ppermute | solution.py:325
  53.7 0.0 collective-permute-done.1.refs_2_
  53.7 0.8 collective-permute-start.6
  54.5 0.0 collective-permute-done.2.refs_3_
  54.5 8.9 %collective-permute-start.7 = (bf16[64,512]{1,0:T(8,128)(2,1)S(1)}, bf16[64,512]{1,0:T(8,128)(2,1)S(1)}, u32[]{:S(2)}, u32[]{:S(2)}) collective-permute-start(bf16[64,512]{1,0:T(8,128)(2,1)S(1)} %slice_bitcast_fusion.7), channel_id=1, source_target_pairs={{0,16},{16,0},{32,48},{48,32},{64,80},{80,64},{96,112},{112,96},{1... | collective-permute-start | bytes 196616 | tf_op jit(solution)/shard_map/ppermute | solution.py:320
  63.4 0.0 collective-permute-done.3.refs_4_
  63.4 1.1 %collective-permute-start.8 = (bf16[64,512]{1,0:T(8,128)(2,1)S(1)}, bf16[64,512]{1,0:T(8,128)(2,1)S(1)}, u32[]{:S(2)}, u32[]{:S(2)}) collective-permute-start(bf16[64,512]{1,0:T(8,128)(2,1)S(1)} %slice_bitcast_fusion.6), channel_id=1, source_target_pairs={{0,16},{16,0},{32,48},{48,32},{64,80},{80,64},{96,112},{112,96},{1... | collective-permute-start | bytes 196616 | tf_op jit(solution)/shard_map/ppermute | solution.py:320
  64.4 0.0 collective-permute-done.4.refs_5_
  64.4 5.7 %collective-permute-start.9 = (bf16[64,512]{1,0:T(8,128)(2,1)S(1)}, bf16[64,512]{1,0:T(8,128)(2,1)S(1)}, u32[]{:S(2)}, u32[]{:S(2)}) collective-permute-start(bf16[64,512]{1,0:T(8,128)(2,1)S(1)} %slice_bitcast_fusion.5), channel_id=1, source_target_pairs={{0,16},{16,0},{32,48},{48,32},{64,80},{80,64},{96,112},{112,96},{1... | collective-permute-start | bytes 196616 | tf_op jit(solution)/shard_map/ppermute | solution.py:320
  70.2 0.7 collective-permute-done.5.refs_6_
  70.9 0.7 collective-permute-start.10
  71.6 0.1 collective-permute-done.6.refs_7_
  71.7 2.2 %collective-permute-start.11 = (bf16[64,512]{1,0:T(8,128)(2,1)S(1)}, bf16[64,512]{1,0:T(8,128)(2,1)S(1)}, u32[]{:S(2)}, u32[]{:S(2)}) collective-permute-start(bf16[64,512]{1,0:T(8,128)(2,1)S(1)} %slice_bitcast_fusion.3), channel_id=1, source_target_pairs={{0,16},{16,0},{32,48},{48,32},{64,80},{80,64},{96,112},{112,96},{1... | collective-permute-start | bytes 196616 | tf_op jit(solution)/shard_map/ppermute | solution.py:320
  73.9 0.0 collective-permute-done.7.refs_8_
  73.9 0.1 collective-permute-start.12
  74.0 0.0 collective-permute-done.8.refs_9_
  74.0 0.5 collective-permute-start.13
  74.5 0.0 collective-permute-done.9.refs_10_
  74.5 0.1 collective-permute-start.14
  74.6 0.0 copy-done.7
  74.6 0.1 copy.10.refs_18_
  74.7 0.0 collective-permute-done.10.refs_11_
  74.7 0.1 collective-permute-done.11.refs_12_
  74.8 0.5 collective-permute-done.12.refs_13_
  75.2 0.2 collective-permute-done.13.refs_14_
  75.4 0.4 collective-permute-done.14.refs_15_
  75.7 0.0 copy-done.4
  75.7 0.0 copy-done.5
  75.8 4.2 %series.1 = (bf16[1,32,64,256]{3,2,1,0:T(8,128)(2,1)}, bf16[256,256]{1,0:T(8,128)(2,1)S(1)}) custom-call(s32[2]{0:T(128)S(1)} %copy-done.6, bf16[2,64,512]{2,1,0:T(8,128)(2,1)S(1)} %get-tuple-element.12.refs_0_, bf16[2,64,512]{2,1,0:T(8,128)(2,1)S(1)} %collective-permute-done.refs_1_, bf16[2,64,512]{2,1,0:T(8,128)(2,1)S(1)} %collective-permute-done.1.refs_2_, ...), custom_call_target="tpu_custom_call" | custom-call | flops 268435456 | bytes 4194304 | tf_op jit(solution)/shard_map/series/pallas_call | solution.py:289
  79.9 10.0 %all_to_all.14 = bf16[16,16,256]{2,1,0:T(8,128)(2,1)S(1)} all-to-all(bf16[16,16,256]{2,1,0:T(8,128)(2,1)S(1)} %bitcast.27), channel_id=1, replica_groups=mesh['freq'=16,'tile'=16] {'tile'}, dimensions={0} | all-to-all | bytes 262144 | tf_op jit(solution)/shard_map/all_to_all | solution.py:348
  90.0 0.6 multiply_bitcast_fusion
  (9 shorter events, 0.1 us)
Async XLA Ops:
  7.1 23.6 %all-to-all-start = ((bf16[16,256,128]{2,1,0:T(8,128)(2,1)}), bf16[16,256,128]{2,1,0:T(8,128)(2,1)S(1)}, u32[]{:S(2)}, u32[]{:S(2)}) async-start(bf16[16,256,128]{2,1,0:T(8,128)(2,1)} %moments.1), calls=%async_computation | async-start | bytes 2097152 | tf_op jit(solution)/shard_map/all_to_all | solution.py:337
  23.8 7.3 %copy-start.6 = (s32[2]{0:T(128)S(1)}, s32[2]{0:T(128)}, u32[]{:S(2)}) copy-start(s32[2]{0:T(128)} %pad_add_fusion.place) | copy-start | bytes 28
  26.8 6.9 %copy-start.2 = (bf16[256,2048]{1,0:T(8,128)(2,1)S(1)}, bf16[256,2048]{1,0:T(8,128)(2,1)}, u32[]{:S(2)}) copy-start(bf16[256,2048]{1,0:T(8,128)(2,1)} %shard_map.97.u_rows) | copy-start | bytes 3145732
  26.8 10.0 %copy-start.1 = (bf16[256,2048]{1,0:T(8,128)(2,1)S(1)}, bf16[256,2048]{1,0:T(8,128)(2,1)}, u32[]{:S(2)}) copy-start(bf16[256,2048]{1,0:T(8,128)(2,1)} %shard_map.99.u_rows) | copy-start | bytes 3145732
  31.2 1.2 %copy-start.3 = (bf16[256,2048]{1,0:T(8,128)(2,1)S(1)}, bf16[256,2048]{1,0:T(8,128)(2,1)}, u32[]{:S(2)}) copy-start(bf16[256,2048]{1,0:T(8,128)(2,1)} %shard_map.95.u_rows) | copy-start | bytes 3145732
  32.4 8.7 %copy-start = (bf16[256,2048]{1,0:T(8,128)(2,1)S(1)}, bf16[256,2048]{1,0:T(8,128)(2,1)}, u32[]{:S(2)}) copy-start(bf16[256,2048]{1,0:T(8,128)(2,1)} %shard_map.101.u_rows) | copy-start | bytes 3145732
  35.0 39.6 %copy-start.7 = (f32[1,64]{1,0:T(1,128)S(1)}, f32[1,64]{1,0:T(1,128)}, u32[]{:S(2)}) copy-start(f32[1,64]{1,0:T(1,128)} %param.15) | copy-start | bytes 772
  35.0 40.7 %copy-start.4 = (bf16[1,32,64,256]{3,2,1,0:T(8,128)(2,1)S(1)}, bf16[1,32,64,256]{3,2,1,0:T(8,128)(2,1)}, u32[]{:S(2)}) copy-start(bf16[1,32,64,256]{3,2,1,0:T(8,128)(2,1)} %refs_16_.1) | copy-start | bytes 3145732
  35.0 40.7 %copy-start.5 = (s32[1,64,256]{2,1,0:T(8,128)S(1)}, s32[1,64,256]{2,1,0:T(8,128)}, u32[]{:S(2)}) copy-start(s32[1,64,256]{2,1,0:T(8,128)} %refs_17_.1) | copy-start | bytes 196612
  35.1 16.1 %collective-permute-start = (bf16[2,64,512]{2,1,0:T(8,128)(2,1)S(1)}, bf16[2,64,512]{2,1,0:T(8,128)(2,1)S(1)}, u32[]{:S(2)}, u32[]{:S(2)}) collective-permute-start(bf16[2,64,512]{2,1,0:T(8,128)(2,1)S(1)} %get-tuple-element.13), channel_id=1, source_target_pairs={{0,32},{16,48},{32,64},{48,80},{64,96},{80,112},{96,128},{112,144}... | collective-permute-start | bytes 393224 | tf_op jit(solution)/shard_map/ppermute | solution.py:325
  38.1 15.6 %collective-permute-start.1 = (bf16[2,64,512]{2,1,0:T(8,128)(2,1)S(1)}, bf16[2,64,512]{2,1,0:T(8,128)(2,1)S(1)}, u32[]{:S(2)}, u32[]{:S(2)}) collective-permute-start(bf16[2,64,512]{2,1,0:T(8,128)(2,1)S(1)} %get-tuple-element.14), channel_id=1, source_target_pairs={{0,64},{16,80},{32,96},{48,112},{64,128},{80,144},{96,160},{112,17... | collective-permute-start | bytes 393224 | tf_op jit(solution)/shard_map/ppermute | solution.py:325
  42.4 12.1 %collective-permute-start.2 = (bf16[2,64,512]{2,1,0:T(8,128)(2,1)S(1)}, bf16[2,64,512]{2,1,0:T(8,128)(2,1)S(1)}, u32[]{:S(2)}, u32[]{:S(2)}) collective-permute-start(bf16[2,64,512]{2,1,0:T(8,128)(2,1)S(1)} %get-tuple-element.15), channel_id=1, source_target_pairs={{0,96},{16,112},{32,128},{48,144},{64,160},{80,176},{96,192},{112,... | collective-permute-start | bytes 393224 | tf_op jit(solution)/shard_map/ppermute | solution.py:325
  46.3 17.1 %collective-permute-start.3 = (bf16[2,64,512]{2,1,0:T(8,128)(2,1)S(1)}, bf16[2,64,512]{2,1,0:T(8,128)(2,1)S(1)}, u32[]{:S(2)}, u32[]{:S(2)}) collective-permute-start(bf16[2,64,512]{2,1,0:T(8,128)(2,1)S(1)} %get-tuple-element.16), channel_id=1, source_target_pairs={{0,128},{16,144},{32,160},{48,176},{64,192},{80,208},{96,224},{112... | collective-permute-start | bytes 393224 | tf_op jit(solution)/shard_map/ppermute | solution.py:325
  46.8 17.6 %collective-permute-start.4 = (bf16[2,64,512]{2,1,0:T(8,128)(2,1)S(1)}, bf16[2,64,512]{2,1,0:T(8,128)(2,1)S(1)}, u32[]{:S(2)}, u32[]{:S(2)}) collective-permute-start(bf16[2,64,512]{2,1,0:T(8,128)(2,1)S(1)} %get-tuple-element.17), channel_id=1, source_target_pairs={{0,160},{16,176},{32,192},{48,208},{64,224},{80,240},{96,0},{112,1... | collective-permute-start | bytes 393224 | tf_op jit(solution)/shard_map/ppermute | solution.py:325
  51.2 19.7 %collective-permute-start.5 = (bf16[2,64,512]{2,1,0:T(8,128)(2,1)S(1)}, bf16[2,64,512]{2,1,0:T(8,128)(2,1)S(1)}, u32[]{:S(2)}, u32[]{:S(2)}) collective-permute-start(bf16[2,64,512]{2,1,0:T(8,128)(2,1)S(1)} %get-tuple-element.18), channel_id=1, source_target_pairs={{0,192},{16,208},{32,224},{48,240},{64,0},{80,16},{96,32},{112,48}... | collective-permute-start | bytes 393224 | tf_op jit(solution)/shard_map/ppermute | solution.py:325
  53.7 18.0 %collective-permute-start.6 = (bf16[2,64,512]{2,1,0:T(8,128)(2,1)S(1)}, bf16[2,64,512]{2,1,0:T(8,128)(2,1)S(1)}, u32[]{:S(2)}, u32[]{:S(2)}) collective-permute-start(bf16[2,64,512]{2,1,0:T(8,128)(2,1)S(1)} %get-tuple-element.19), channel_id=1, source_target_pairs={{0,224},{16,240},{32,0},{48,16},{64,32},{80,48},{96,64},{112,80},{... | collective-permute-start | bytes 393224 | tf_op jit(solution)/shard_map/ppermute | solution.py:325
  54.5 19.4 %collective-permute-start.7 = (bf16[64,512]{1,0:T(8,128)(2,1)S(1)}, bf16[64,512]{1,0:T(8,128)(2,1)S(1)}, u32[]{:S(2)}, u32[]{:S(2)}) collective-permute-start(bf16[64,512]{1,0:T(8,128)(2,1)S(1)} %slice_bitcast_fusion.7), channel_id=1, source_target_pairs={{0,16},{16,0},{32,48},{48,32},{64,80},{80,64},{96,112},{112,96},{1... | collective-permute-start | bytes 196616 | tf_op jit(solution)/shard_map/ppermute | solution.py:320
  63.4 10.6 %collective-permute-start.8 = (bf16[64,512]{1,0:T(8,128)(2,1)S(1)}, bf16[64,512]{1,0:T(8,128)(2,1)S(1)}, u32[]{:S(2)}, u32[]{:S(2)}) collective-permute-start(bf16[64,512]{1,0:T(8,128)(2,1)S(1)} %slice_bitcast_fusion.6), channel_id=1, source_target_pairs={{0,16},{16,0},{32,48},{48,32},{64,80},{80,64},{96,112},{112,96},{1... | collective-permute-start | bytes 196616 | tf_op jit(solution)/shard_map/ppermute | solution.py:320
  64.4 10.1 %collective-permute-start.9 = (bf16[64,512]{1,0:T(8,128)(2,1)S(1)}, bf16[64,512]{1,0:T(8,128)(2,1)S(1)}, u32[]{:S(2)}, u32[]{:S(2)}) collective-permute-start(bf16[64,512]{1,0:T(8,128)(2,1)S(1)} %slice_bitcast_fusion.5), channel_id=1, source_target_pairs={{0,16},{16,0},{32,48},{48,32},{64,80},{80,64},{96,112},{112,96},{1... | collective-permute-start | bytes 196616 | tf_op jit(solution)/shard_map/ppermute | solution.py:320
  70.9 3.8 %collective-permute-start.10 = (bf16[64,512]{1,0:T(8,128)(2,1)S(1)}, bf16[64,512]{1,0:T(8,128)(2,1)S(1)}, u32[]{:S(2)}, u32[]{:S(2)}) collective-permute-start(bf16[64,512]{1,0:T(8,128)(2,1)S(1)} %slice_bitcast_fusion.4), channel_id=1, source_target_pairs={{0,16},{16,0},{32,48},{48,32},{64,80},{80,64},{96,112},{112,96},{1... | collective-permute-start | bytes 196616 | tf_op jit(solution)/shard_map/ppermute | solution.py:320
  71.7 3.1 %collective-permute-start.11 = (bf16[64,512]{1,0:T(8,128)(2,1)S(1)}, bf16[64,512]{1,0:T(8,128)(2,1)S(1)}, u32[]{:S(2)}, u32[]{:S(2)}) collective-permute-start(bf16[64,512]{1,0:T(8,128)(2,1)S(1)} %slice_bitcast_fusion.3), channel_id=1, source_target_pairs={{0,16},{16,0},{32,48},{48,32},{64,80},{80,64},{96,112},{112,96},{1... | collective-permute-start | bytes 196616 | tf_op jit(solution)/shard_map/ppermute | solution.py:320
  73.9 1.3 %collective-permute-start.12 = (bf16[64,512]{1,0:T(8,128)(2,1)S(1)}, bf16[64,512]{1,0:T(8,128)(2,1)S(1)}, u32[]{:S(2)}, u32[]{:S(2)}) collective-permute-start(bf16[64,512]{1,0:T(8,128)(2,1)S(1)} %slice_bitcast_fusion.2), channel_id=1, source_target_pairs={{0,16},{16,0},{32,48},{48,32},{64,80},{80,64},{96,112},{112,96},{1... | collective-permute-start | bytes 196616 | tf_op jit(solution)/shard_map/ppermute | solution.py:320
  74.0 1.4 %collective-permute-start.13 = (bf16[64,512]{1,0:T(8,128)(2,1)S(1)}, bf16[64,512]{1,0:T(8,128)(2,1)S(1)}, u32[]{:S(2)}, u32[]{:S(2)}) collective-permute-start(bf16[64,512]{1,0:T(8,128)(2,1)S(1)} %slice_bitcast_fusion.1), channel_id=1, source_target_pairs={{0,16},{16,0},{32,48},{48,32},{64,80},{80,64},{96,112},{112,96},{1... | collective-permute-start | bytes 196616 | tf_op jit(solution)/shard_map/ppermute | solution.py:320
  74.5 1.3 %collective-permute-start.14 = (bf16[64,512]{1,0:T(8,128)(2,1)S(1)}, bf16[64,512]{1,0:T(8,128)(2,1)S(1)}, u32[]{:S(2)}, u32[]{:S(2)}) collective-permute-start(bf16[64,512]{1,0:T(8,128)(2,1)S(1)} %slice_bitcast_fusion), channel_id=1, source_target_pairs={{0,16},{16,0},{32,48},{48,32},{64,80},{80,64},{96,112},{112,96},{1... | collective-permute-start | bytes 196616 | tf_op jit(solution)/shard_map/ppermute | solution.py:320

commit v3 on v2

--- a/solution.py
+++ b/solution.py
@@ -121,21 +121,21 @@
     )(place, u_tiles)
 
 
-def terms_kernel(received, terms):
+def terms_kernel(received, terms, *, scale):
     tiles, focal, wide = received.shape
     lane = lax.broadcasted_iota(jnp.int32, (focal, wide), 1)
     sign = jnp.where(lane < wide // 2, 1.0, -1.0)
     for j in range(tiles):
-        coeffs = received[j].astype(jnp.float32)
+        coeffs = received[j].astype(jnp.float32) * scale
         at = slice(j * wide, (j + 1) * wide)
         terms[:focal, at] = (coeffs * sign).astype(jnp.bfloat16)
         terms[focal:, at] = pltpu.roll(coeffs, wide // 2, 1).astype(jnp.bfloat16)
 
 
-def rank_terms(received):
+def rank_terms(received, scale):
     tiles, focal, wide = received.shape
     return pl.pallas_call(
-        terms_kernel,
+        functools.partial(terms_kernel, scale=scale),
         in_specs=[spec()],
         out_specs=spec(),
         out_shape=jax.ShapeDtypeStruct((2 * focal, tiles * wide), jnp.bfloat16),
@@ -145,9 +145,13 @@
     )(received)
 
 
-def fields_kernel(place, terms, u_rows, *outs):
+def fields_kernel(terms, u_rows, *outs):
+    fields_of(terms, u_rows, outs)
+
+
+def fields_of(terms, u_rows, outs):
     sub = outs[0].shape[1]
-    core = place[1]
+    core = lax.rem(lax.axis_index("freq"), 2)
     product = lax.dot_general(
         u_rows[...], terms[...], (((1,), (1,)), ((), ())), preferred_element_type=jnp.float32
     ).astype(jnp.bfloat16)
@@ -157,20 +161,20 @@
         out[1 - core] = product[base + sub : base + 2 * sub]
 
 
-def fields(place, terms, u_rows, distances):
+def fields(terms, u_rows, distances):
     rows, depth = u_rows.shape
     wide = terms.shape[0]
     sub = rows // (2 * len(distances))
     return pl.pallas_call(
         fields_kernel,
-        in_specs=[pl.BlockSpec(memory_space=pltpu.SMEM), spec(), spec()],
+        in_specs=[spec(), spec()],
         out_specs=[spec()] * len(distances),
         out_shape=[jax.ShapeDtypeStruct((2, sub, wide), jnp.bfloat16)] * len(distances),
         cost_estimate=pl.CostEstimate(
             flops=2 * rows * depth * wide, bytes_accessed=3 << 20, transcendentals=0
         ),
         compiler_params=pltpu.CompilerParams(vmem_limit_bytes=14 << 20),
-    )(place, terms, u_rows)
+    )(terms, u_rows)
 
 
 def halves(terms, kind, period):
@@ -231,18 +235,18 @@
     return out
 
 
-def series_kernel(place, *refs, chips, steps):
+def series_kernel(*refs, chips, steps, scale):
     own, swapped = refs[:chips], refs[chips : 2 * chips]
     initial, mutes, taper, focusing, partial, spectra, signal, weighted, total = refs[2 * chips :]
     step = pl.program_id(0)
-    chip, core = place[0], place[1]
+    me = lax.axis_index("freq")
+    chip, core = lax.div(me, 2), lax.rem(me, 2)
     trace, rows, focal = initial.shape
     freqs = 2 * chips
-    scale = 1.0 / math.sqrt(freqs)
     for d in range(chips):
         source = 2 * lax.rem(chip + chips - d, chips)
         for value, f in ((own[d][...], source + core), (swapped[d][...], source + 1 - core)):
-            value = value.astype(jnp.float32) * scale
+            value = value.astype(jnp.float32)
             spectra[f, 0] = value[:, :focal]
             spectra[f, 1] = value[:, focal:]
     for r in range(rows // 8):
@@ -278,19 +282,18 @@
 
     @pl.when(step == steps - 1)
     def _():
-        partial[...] = total[...].astype(jnp.bfloat16)
-
-
-def series_update(place, own, swapped, initial, mutes, taper, rows=16):
+        partial[...] = (total[...] * scale).astype(jnp.bfloat16)
+
+
+def series_update(own, swapped, initial, mutes, taper, scale, rows=16):
     chips = len(own)
     _, trace, sub, focal = initial.shape
     steps = sub // rows
     times = spec((None, trace, rows, focal), lambda s: (0, 0, s, 0))
     return pl.pallas_call(
-        functools.partial(series_kernel, chips=chips, steps=steps),
+        functools.partial(series_kernel, chips=chips, steps=steps, scale=scale),
         grid=(steps,),
-        in_specs=[pl.BlockSpec(memory_space=pltpu.SMEM)]
-        + [spec((None, rows, 2 * focal), lambda s: (0, s, 0))] * chips
+        in_specs=[spec((None, rows, 2 * focal), lambda s: (0, s, 0))] * chips
         + [spec((rows, 2 * focal), lambda s: (s, 0))] * chips
         + [
             times,
@@ -313,7 +316,7 @@
         ),
         compiler_params=pltpu.CompilerParams(vmem_limit_bytes=14 << 20),
         name="series",
-    )(place, *own, *swapped, initial, mutes, taper)
+    )(*own, *swapped, initial, mutes, taper)
 
 
 def swap_cores(values, freq_count):
@@ -335,24 +338,22 @@
     u_rows = [flatten(place, u_factors[0], distances, chips) for distances in ORDER]
     coeffs = moments(ranks[0, :, 0], tile_mask[0, :, 0], focal_field[0], v_factors[0])
     received = lax.all_to_all(coeffs, "tile", split_axis=0, concat_axis=0, tiled=True)
-    terms = rank_terms(received)
+    terms = rank_terms(received, 1.0 / math.sqrt(freq_count))
     own, swapped = [None] * chips, [None] * chips
     for n, distances in enumerate(ORDER):
-        blocks = fields(place, terms, u_rows[n], distances)
+        blocks = fields(terms, u_rows[n], distances)
         for d, block in zip(distances, blocks):
             own[d] = shift_chips(block, d, freq_count) if d else block
             swapped[d] = swap_cores(own[d][1], freq_count)
+    trace_length, group_rows = initial_focus.shape[1:3]
+    normalizer = 1.0 / float(tile_count * trace_length * group_rows)
     focusing, partial = series_update(
-        place, own, swapped, initial_focus, mute_starts, taper[0][:, None]
+        own, swapped, initial_focus, mute_starts, taper[0][:, None], normalizer
     )
     shares = lax.all_to_all(partial, "tile", split_axis=0, concat_axis=0, tiled=True)
-    trace_length, group_rows = initial_focus.shape[1:3]
-    normalizer = 1.0 / float(tile_count * trace_length * group_rows)
     share_rows = focal_count // tile_count
-    own_rows = jnp.sum(
-        shares.reshape(tile_count, share_rows, focal_count).astype(jnp.float32), axis=0
-    )
-    return (focusing, (own_rows * normalizer)[None])
+    shares = shares.reshape(tile_count, 1, share_rows, focal_count)
+    return (focusing, jnp.sum(shares.astype(jnp.float32), axis=0))
 
 
 def solution(mesh):

time: 91.9 us -> 89.1 us (0.970)
  Pallas kernels: 27.6 us -> 24.7 us
    pallas_call x6, Pallas kernels: 9.72 us -> 6.95 us  [the longest x1 3.52 us: series_update(): pl.pallas_call(functools.partial(series_kernel, chips=chips, steps=steps,...]
where the time goes in v3:
time: 89.1 us; the launch traced here: 87.8 us
  starting transfers between devices  43.6 us (49%)
  Pallas kernels  24.7 us (28%)
  blocking collectives  10 us (11%)
  waiting for transfers between devices  6 us (7%)
  local copies, waits for them, and re-layouts  1.39 us (2%)
  other arithmetic  1.27 us (1%)
    ppermute x8, starting transfers between devices, swap_cores(): return lax.ppermute(values, 'freq', [(f, f ^ 1) for f in range(freq_count)])  19.2 us
    ppermute x7, starting transfers between devices, shift_chips(): return lax.ppermute(values, 'freq', pairs)  16.8 us
    pallas_call x4, Pallas kernels, flatten(): pl.pallas_call(flatten_kernel, grid_spec=pltpu.PrefetchScalarGridSpec(num...  11.3 us
    all_to_all x1, blocking collectives, update(): lax.all_to_all(partial, 'tile', split_axis=0, concat_axis=0, tiled=True)  10 us
    all_to_all x1, starting transfers between devices, update(): lax.all_to_all(coeffs, 'tile', split_axis=0, concat_axis=0, tiled=True)  7.58 us
    pallas_call x1, Pallas kernels, moments(): pl.pallas_call(moments_kernel, in_specs=[pl.BlockSpec(memory_space=pltpu....  6.48 us
    all_to_all x1, waiting for transfers between devices, update(): lax.all_to_all(coeffs, 'tile', split_axis=0, concat_axis=0, tiled=True)  4.11 us
    pallas_call x1, Pallas kernels, series_update(): pl.pallas_call(functools.partial(series_kernel, chips=chips, steps=steps,...  3.52 us
  transfers between devices with their start and end apart: 16, of which 7 were waited for; matrix products, arithmetic and copies ran while one was open for 1% of the time, Pallas kernels for 15%

profile of v3, /device:TPU:1, one launch (start us, length us, event | category | flops | bytes accessed | tf_op | source)
XLA Modules:
  0.0 87.8 jit_solution(4026098310271013888)
XLA Ops:
  0.6 6.5 %moments.1 = bf16[16,256,128]{2,1,0:T(8,128)(2,1)} custom-call(s32[16]{0:T(128)} %bitcast.35, s32[16]{0:T(128)} %bitcast.36, bf16[1024,2,256]{2,1,0:T(2,128)(2,1)} %bitcast.34, bf16[16,1024,128]{2,1,0:T(8,128)(2,1)} %bitcast.33), custom_call_target="tpu_custom_call" | custom-call | flops 2147483648 | bytes 6291456 | tf_op jit(solution)/shard_map/moments/pallas_call | solution.py:73
  7.1 7.6 %all-to-all-start = ((bf16[16,256,128]{2,1,0:T(8,128)(2,1)}), bf16[16,256,128]{2,1,0:T(8,128)(2,1)S(1)}, u32[]{:S(2)}, u32[]{:S(2)}) async-start(bf16[16,256,128]{2,1,0:T(8,128)(2,1)} %moments.1), calls=%async_computation | async-start | bytes 2097152 | tf_op jit(solution)/shard_map/all_to_all | solution.py:340
  14.7 0.6 pad_add_fusion.place
  15.4 2.9 %shard_map.95.u_rows = bf16[256,2048]{1,0:T(8,128)(2,1)} custom-call(s32[2]{0:T(128)} %pad_add_fusion.place, bf16[1024,16,128]{2,1,0:T(8,128)(2,1)} %bitcast.27), custom_call_target="tpu_custom_call" | custom-call | flops 4194304 | bytes 8388608 | tf_op jit(solution)/shard_map/pallas_call | solution.py:110
  18.2 2.8 %shard_map.97.u_rows = bf16[256,2048]{1,0:T(8,128)(2,1)} custom-call(s32[2]{0:T(128)} %pad_add_fusion.place, bf16[1024,16,128]{2,1,0:T(8,128)(2,1)} %bitcast.28), custom_call_target="tpu_custom_call" | custom-call | flops 4194304 | bytes 8388608 | tf_op jit(solution)/shard_map/pallas_call | solution.py:110
  21.0 2.8 %shard_map.99.u_rows = bf16[256,2048]{1,0:T(8,128)(2,1)} custom-call(s32[2]{0:T(128)} %pad_add_fusion.place, bf16[1024,16,128]{2,1,0:T(8,128)(2,1)} %bitcast.29), custom_call_target="tpu_custom_call" | custom-call | flops 4194304 | bytes 8388608 | tf_op jit(solution)/shard_map/pallas_call | solution.py:110
  23.8 2.8 %shard_map.101.u_rows = bf16[256,2048]{1,0:T(8,128)(2,1)} custom-call(s32[2]{0:T(128)} %pad_add_fusion.place, bf16[1024,16,128]{2,1,0:T(8,128)(2,1)} %bitcast.30), custom_call_target="tpu_custom_call" | custom-call | flops 4194304 | bytes 8388608 | tf_op jit(solution)/shard_map/pallas_call | solution.py:110
  26.6 0.0 copy-start.2
  26.6 0.0 copy-start.1
  26.6 4.1 %all-to-all-done.received = bf16[16,256,128]{2,1,0:T(8,128)(2,1)S(1)} async-done(((bf16[16,256,128]{2,1,0:T(8,128)(2,1)}), bf16[16,256,128]{2,1,0:T(8,128)(2,1)S(1)}, u32[]{:S(2)}, u32[]{:S(2)}) %all-to-all-start) | async-done | bytes 1048608 | tf_op jit(solution)/shard_map/all_to_all | solution.py:340
  30.7 0.5 terms.1
  31.2 0.0 copy-start.3
  31.3 1.2 %copy-done.3 = bf16[256,2048]{1,0:T(8,128)(2,1)S(1)} copy-done((bf16[256,2048]{1,0:T(8,128)(2,1)S(1)}, bf16[256,2048]{1,0:T(8,128)(2,1)}, u32[]{:S(2)}) %copy-start.3) | copy-done | bytes 1048600
  32.5 0.0 copy-start
  32.5 0.7 shard_map.96
  33.2 0.0 copy-done.2
  33.2 0.7 shard_map.98
  34.0 0.0 copy-start.6
  34.0 0.0 copy-start.4
  34.0 0.0 copy-start.5
  34.0 1.7 %collective-permute-start = (bf16[2,64,512]{2,1,0:T(8,128)(2,1)S(1)}, bf16[2,64,512]{2,1,0:T(8,128)(2,1)S(1)}, u32[]{:S(2)}, u32[]{:S(2)}) collective-permute-start(bf16[2,64,512]{2,1,0:T(8,128)(2,1)S(1)} %get-tuple-element.13), channel_id=1, source_target_pairs={{0,32},{16,48},{32,64},{48,80},{64,96},{80,112},{96,128},{112,144}... | collective-permute-start | bytes 393224 | tf_op jit(solution)/shard_map/ppermute | solution.py:328
  35.7 0.0 copy-done.1
  35.7 0.7 shard_map.100
  36.5 3.1 %collective-permute-start.1 = (bf16[2,64,512]{2,1,0:T(8,128)(2,1)S(1)}, bf16[2,64,512]{2,1,0:T(8,128)(2,1)S(1)}, u32[]{:S(2)}, u32[]{:S(2)}) collective-permute-start(bf16[2,64,512]{2,1,0:T(8,128)(2,1)S(1)} %get-tuple-element.14), channel_id=1, source_target_pairs={{0,64},{16,80},{32,96},{48,112},{64,128},{80,144},{96,160},{112,17... | collective-permute-start | bytes 393224 | tf_op jit(solution)/shard_map/ppermute | solution.py:328
  39.5 0.0 copy-done
  39.5 0.7 shard_map.102
  40.3 3.8 %collective-permute-start.2 = (bf16[2,64,512]{2,1,0:T(8,128)(2,1)S(1)}, bf16[2,64,512]{2,1,0:T(8,128)(2,1)S(1)}, u32[]{:S(2)}, u32[]{:S(2)}) collective-permute-start(bf16[2,64,512]{2,1,0:T(8,128)(2,1)S(1)} %get-tuple-element.15), channel_id=1, source_target_pairs={{0,96},{16,112},{32,128},{48,144},{64,160},{80,176},{96,192},{112,... | collective-permute-start | bytes 393224 | tf_op jit(solution)/shard_map/ppermute | solution.py:328
  44.1 0.5 collective-permute-start.3
  44.7 4.4 %collective-permute-start.4 = (bf16[2,64,512]{2,1,0:T(8,128)(2,1)S(1)}, bf16[2,64,512]{2,1,0:T(8,128)(2,1)S(1)}, u32[]{:S(2)}, u32[]{:S(2)}) collective-permute-start(bf16[2,64,512]{2,1,0:T(8,128)(2,1)S(1)} %get-tuple-element.17), channel_id=1, source_target_pairs={{0,160},{16,176},{32,192},{48,208},{64,224},{80,240},{96,0},{112,1... | collective-permute-start | bytes 393224 | tf_op jit(solution)/shard_map/ppermute | solution.py:328
  49.1 0.0 collective-permute-done.refs_1_
  49.1 2.5 %collective-permute-start.5 = (bf16[2,64,512]{2,1,0:T(8,128)(2,1)S(1)}, bf16[2,64,512]{2,1,0:T(8,128)(2,1)S(1)}, u32[]{:S(2)}, u32[]{:S(2)}) collective-permute-start(bf16[2,64,512]{2,1,0:T(8,128)(2,1)S(1)} %get-tuple-element.18), channel_id=1, source_target_pairs={{0,192},{16,208},{32,224},{48,240},{64,0},{80,16},{96,32},{112,48}... | collective-permute-start | bytes 393224 | tf_op jit(solution)/shard_map/ppermute | solution.py:328
  51.5 0.0 collective-permute-done.1.refs_2_
  51.5 0.8 collective-permute-start.6
  52.3 0.0 collective-permute-done.2.refs_3_
  52.4 10.2 %collective-permute-start.7 = (bf16[64,512]{1,0:T(8,128)(2,1)S(1)}, bf16[64,512]{1,0:T(8,128)(2,1)S(1)}, u32[]{:S(2)}, u32[]{:S(2)}) collective-permute-start(bf16[64,512]{1,0:T(8,128)(2,1)S(1)} %slice_bitcast_fusion.7), channel_id=1, source_target_pairs={{0,16},{16,0},{32,48},{48,32},{64,80},{80,64},{96,112},{112,96},{1... | collective-permute-start | bytes 196616 | tf_op jit(solution)/shard_map/ppermute | solution.py:323
  62.5 0.0 collective-permute-done.3.refs_4_
  62.5 0.7 collective-permute-start.8
  63.2 0.0 collective-permute-done.4.refs_5_
  63.2 4.8 %collective-permute-start.9 = (bf16[64,512]{1,0:T(8,128)(2,1)S(1)}, bf16[64,512]{1,0:T(8,128)(2,1)S(1)}, u32[]{:S(2)}, u32[]{:S(2)}) collective-permute-start(bf16[64,512]{1,0:T(8,128)(2,1)S(1)} %slice_bitcast_fusion.5), channel_id=1, source_target_pairs={{0,16},{16,0},{32,48},{48,32},{64,80},{80,64},{96,112},{112,96},{1... | collective-permute-start | bytes 196616 | tf_op jit(solution)/shard_map/ppermute | solution.py:323
  68.1 0.7 collective-permute-done.5.refs_6_
  68.7 0.7 collective-permute-start.10
  69.4 0.1 collective-permute-done.6.refs_7_
  69.6 2.2 %collective-permute-start.11 = (bf16[64,512]{1,0:T(8,128)(2,1)S(1)}, bf16[64,512]{1,0:T(8,128)(2,1)S(1)}, u32[]{:S(2)}, u32[]{:S(2)}) collective-permute-start(bf16[64,512]{1,0:T(8,128)(2,1)S(1)} %slice_bitcast_fusion.3), channel_id=1, source_target_pairs={{0,16},{16,0},{32,48},{48,32},{64,80},{80,64},{96,112},{112,96},{1... | collective-permute-start | bytes 196616 | tf_op jit(solution)/shard_map/ppermute | solution.py:323
  71.7 0.0 collective-permute-done.7.refs_8_
  71.8 0.1 collective-permute-start.12
  71.9 0.0 collective-permute-done.8.refs_9_
  71.9 0.5 collective-permute-start.13
  72.4 0.0 collective-permute-done.9.refs_10_
  72.4 0.1 collective-permute-start.14
  72.5 0.0 copy-done.6
  72.5 0.1 copy.10.refs_18_
  72.6 0.0 collective-permute-done.10.refs_11_
  72.6 0.1 collective-permute-done.11.refs_12_
  72.6 0.5 collective-permute-done.12.refs_13_
  73.1 0.2 collective-permute-done.13.refs_14_
  73.3 0.4 collective-permute-done.14.refs_15_
  73.6 0.0 copy-done.4
  73.6 0.0 copy-done.5
  73.6 3.5 %series.1 = (bf16[1,32,64,256]{3,2,1,0:T(8,128)(2,1)}, bf16[256,256]{1,0:T(8,128)(2,1)S(1)}) custom-call(bf16[2,64,512]{2,1,0:T(8,128)(2,1)S(1)} %get-tuple-element.12.refs_0_, bf16[2,64,512]{2,1,0:T(8,128)(2,1)S(1)} %collective-permute-done.refs_1_, bf16[2,64,512]{2,1,0:T(8,128)(2,1)S(1)} %collective-permute-done.1.refs_2_, ...), custom_call_target="tpu_custom_call" | custom-call | flops 268435456 | bytes 4194304 | tf_op jit(solution)/shard_map/series/pallas_call | solution.py:293
  77.1 10.0 %all_to_all.14 = bf16[16,16,256]{2,1,0:T(8,128)(2,1)S(1)} all-to-all(bf16[16,16,256]{2,1,0:T(8,128)(2,1)S(1)} %bitcast.26), channel_id=1, replica_groups=mesh['freq'=16,'tile'=16] {'tile'}, dimensions={0} | all-to-all | bytes 262144 | tf_op jit(solution)/shard_map/all_to_all | solution.py:353
  87.2 0.6 convert_reduce_fusion
  (8 shorter events, 0.0 us)
Async XLA Ops:
  7.1 23.6 %all-to-all-start = ((bf16[16,256,128]{2,1,0:T(8,128)(2,1)}), bf16[16,256,128]{2,1,0:T(8,128)(2,1)S(1)}, u32[]{:S(2)}, u32[]{:S(2)}) async-start(bf16[16,256,128]{2,1,0:T(8,128)(2,1)} %moments.1), calls=%async_computation | async-start | bytes 2097152 | tf_op jit(solution)/shard_map/all_to_all | solution.py:340
  26.6 6.6 %copy-start.2 = (bf16[256,2048]{1,0:T(8,128)(2,1)S(1)}, bf16[256,2048]{1,0:T(8,128)(2,1)}, u32[]{:S(2)}) copy-start(bf16[256,2048]{1,0:T(8,128)(2,1)} %shard_map.97.u_rows) | copy-start | bytes 3145732
  26.6 9.1 %copy-start.1 = (bf16[256,2048]{1,0:T(8,128)(2,1)S(1)}, bf16[256,2048]{1,0:T(8,128)(2,1)}, u32[]{:S(2)}) copy-start(bf16[256,2048]{1,0:T(8,128)(2,1)} %shard_map.99.u_rows) | copy-start | bytes 3145732
  31.2 1.2 %copy-start.3 = (bf16[256,2048]{1,0:T(8,128)(2,1)S(1)}, bf16[256,2048]{1,0:T(8,128)(2,1)}, u32[]{:S(2)}) copy-start(bf16[256,2048]{1,0:T(8,128)(2,1)} %shard_map.95.u_rows) | copy-start | bytes 3145732
  32.5 7.1 %copy-start = (bf16[256,2048]{1,0:T(8,128)(2,1)S(1)}, bf16[256,2048]{1,0:T(8,128)(2,1)}, u32[]{:S(2)}) copy-start(bf16[256,2048]{1,0:T(8,128)(2,1)} %shard_map.101.u_rows) | copy-start | bytes 3145732
  34.0 38.5 %copy-start.6 = (f32[1,64]{1,0:T(1,128)S(1)}, f32[1,64]{1,0:T(1,128)}, u32[]{:S(2)}) copy-start(f32[1,64]{1,0:T(1,128)} %param.15) | copy-start | bytes 772
  34.0 39.6 %copy-start.4 = (bf16[1,32,64,256]{3,2,1,0:T(8,128)(2,1)S(1)}, bf16[1,32,64,256]{3,2,1,0:T(8,128)(2,1)}, u32[]{:S(2)}) copy-start(bf16[1,32,64,256]{3,2,1,0:T(8,128)(2,1)} %refs_16_.1) | copy-start | bytes 3145732
  34.0 39.6 %copy-start.5 = (s32[1,64,256]{2,1,0:T(8,128)S(1)}, s32[1,64,256]{2,1,0:T(8,128)}, u32[]{:S(2)}) copy-start(s32[1,64,256]{2,1,0:T(8,128)} %refs_17_.1) | copy-start | bytes 196612
  34.0 15.0 %collective-permute-start = (bf16[2,64,512]{2,1,0:T(8,128)(2,1)S(1)}, bf16[2,64,512]{2,1,0:T(8,128)(2,1)S(1)}, u32[]{:S(2)}, u32[]{:S(2)}) collective-permute-start(bf16[2,64,512]{2,1,0:T(8,128)(2,1)S(1)} %get-tuple-element.13), channel_id=1, source_target_pairs={{0,32},{16,48},{32,64},{48,80},{64,96},{80,112},{96,128},{112,144}... | collective-permute-start | bytes 393224 | tf_op jit(solution)/shard_map/ppermute | solution.py:328
  36.5 15.1 %collective-permute-start.1 = (bf16[2,64,512]{2,1,0:T(8,128)(2,1)S(1)}, bf16[2,64,512]{2,1,0:T(8,128)(2,1)S(1)}, u32[]{:S(2)}, u32[]{:S(2)}) collective-permute-start(bf16[2,64,512]{2,1,0:T(8,128)(2,1)S(1)} %get-tuple-element.14), channel_id=1, source_target_pairs={{0,64},{16,80},{32,96},{48,112},{64,128},{80,144},{96,160},{112,17... | collective-permute-start | bytes 393224 | tf_op jit(solution)/shard_map/ppermute | solution.py:328
  40.3 12.1 %collective-permute-start.2 = (bf16[2,64,512]{2,1,0:T(8,128)(2,1)S(1)}, bf16[2,64,512]{2,1,0:T(8,128)(2,1)S(1)}, u32[]{:S(2)}, u32[]{:S(2)}) collective-permute-start(bf16[2,64,512]{2,1,0:T(8,128)(2,1)S(1)} %get-tuple-element.15), channel_id=1, source_target_pairs={{0,96},{16,112},{32,128},{48,144},{64,160},{80,176},{96,192},{112,... | collective-permute-start | bytes 393224 | tf_op jit(solution)/shard_map/ppermute | solution.py:328
  44.1 18.4 %collective-permute-start.3 = (bf16[2,64,512]{2,1,0:T(8,128)(2,1)S(1)}, bf16[2,64,512]{2,1,0:T(8,128)(2,1)S(1)}, u32[]{:S(2)}, u32[]{:S(2)}) collective-permute-start(bf16[2,64,512]{2,1,0:T(8,128)(2,1)S(1)} %get-tuple-element.16), channel_id=1, source_target_pairs={{0,128},{16,144},{32,160},{48,176},{64,192},{80,208},{96,224},{112... | collective-permute-start | bytes 393224 | tf_op jit(solution)/shard_map/ppermute | solution.py:328
  44.7 18.6 %collective-permute-start.4 = (bf16[2,64,512]{2,1,0:T(8,128)(2,1)S(1)}, bf16[2,64,512]{2,1,0:T(8,128)(2,1)S(1)}, u32[]{:S(2)}, u32[]{:S(2)}) collective-permute-start(bf16[2,64,512]{2,1,0:T(8,128)(2,1)S(1)} %get-tuple-element.17), channel_id=1, source_target_pairs={{0,160},{16,176},{32,192},{48,208},{64,224},{80,240},{96,0},{112,1... | collective-permute-start | bytes 393224 | tf_op jit(solution)/shard_map/ppermute | solution.py:328
  49.1 19.7 %collective-permute-start.5 = (bf16[2,64,512]{2,1,0:T(8,128)(2,1)S(1)}, bf16[2,64,512]{2,1,0:T(8,128)(2,1)S(1)}, u32[]{:S(2)}, u32[]{:S(2)}) collective-permute-start(bf16[2,64,512]{2,1,0:T(8,128)(2,1)S(1)} %get-tuple-element.18), channel_id=1, source_target_pairs={{0,192},{16,208},{32,224},{48,240},{64,0},{80,16},{96,32},{112,48}... | collective-permute-start | bytes 393224 | tf_op jit(solution)/shard_map/ppermute | solution.py:328
  51.5 18.0 %collective-permute-start.6 = (bf16[2,64,512]{2,1,0:T(8,128)(2,1)S(1)}, bf16[2,64,512]{2,1,0:T(8,128)(2,1)S(1)}, u32[]{:S(2)}, u32[]{:S(2)}) collective-permute-start(bf16[2,64,512]{2,1,0:T(8,128)(2,1)S(1)} %get-tuple-element.19), channel_id=1, source_target_pairs={{0,224},{16,240},{32,0},{48,16},{64,32},{80,48},{96,64},{112,80},{... | collective-permute-start | bytes 393224 | tf_op jit(solution)/shard_map/ppermute | solution.py:328
  52.4 19.4 %collective-permute-start.7 = (bf16[64,512]{1,0:T(8,128)(2,1)S(1)}, bf16[64,512]{1,0:T(8,128)(2,1)S(1)}, u32[]{:S(2)}, u32[]{:S(2)}) collective-permute-start(bf16[64,512]{1,0:T(8,128)(2,1)S(1)} %slice_bitcast_fusion.7), channel_id=1, source_target_pairs={{0,16},{16,0},{32,48},{48,32},{64,80},{80,64},{96,112},{112,96},{1... | collective-permute-start | bytes 196616 | tf_op jit(solution)/shard_map/ppermute | solution.py:323
  62.5 9.3 %collective-permute-start.8 = (bf16[64,512]{1,0:T(8,128)(2,1)S(1)}, bf16[64,512]{1,0:T(8,128)(2,1)S(1)}, u32[]{:S(2)}, u32[]{:S(2)}) collective-permute-start(bf16[64,512]{1,0:T(8,128)(2,1)S(1)} %slice_bitcast_fusion.6), channel_id=1, source_target_pairs={{0,16},{16,0},{32,48},{48,32},{64,80},{80,64},{96,112},{112,96},{1... | collective-permute-start | bytes 196616 | tf_op jit(solution)/shard_map/ppermute | solution.py:323
  63.2 9.1 %collective-permute-start.9 = (bf16[64,512]{1,0:T(8,128)(2,1)S(1)}, bf16[64,512]{1,0:T(8,128)(2,1)S(1)}, u32[]{:S(2)}, u32[]{:S(2)}) collective-permute-start(bf16[64,512]{1,0:T(8,128)(2,1)S(1)} %slice_bitcast_fusion.5), channel_id=1, source_target_pairs={{0,16},{16,0},{32,48},{48,32},{64,80},{80,64},{96,112},{112,96},{1... | collective-permute-start | bytes 196616 | tf_op jit(solution)/shard_map/ppermute | solution.py:323
  68.7 3.8 %collective-permute-start.10 = (bf16[64,512]{1,0:T(8,128)(2,1)S(1)}, bf16[64,512]{1,0:T(8,128)(2,1)S(1)}, u32[]{:S(2)}, u32[]{:S(2)}) collective-permute-start(bf16[64,512]{1,0:T(8,128)(2,1)S(1)} %slice_bitcast_fusion.4), channel_id=1, source_target_pairs={{0,16},{16,0},{32,48},{48,32},{64,80},{80,64},{96,112},{112,96},{1... | collective-permute-start | bytes 196616 | tf_op jit(solution)/shard_map/ppermute | solution.py:323
  69.6 3.1 %collective-permute-start.11 = (bf16[64,512]{1,0:T(8,128)(2,1)S(1)}, bf16[64,512]{1,0:T(8,128)(2,1)S(1)}, u32[]{:S(2)}, u32[]{:S(2)}) collective-permute-start(bf16[64,512]{1,0:T(8,128)(2,1)S(1)} %slice_bitcast_fusion.3), channel_id=1, source_target_pairs={{0,16},{16,0},{32,48},{48,32},{64,80},{80,64},{96,112},{112,96},{1... | collective-permute-start | bytes 196616 | tf_op jit(solution)/shard_map/ppermute | solution.py:323
  71.8 1.3 %collective-permute-start.12 = (bf16[64,512]{1,0:T(8,128)(2,1)S(1)}, bf16[64,512]{1,0:T(8,128)(2,1)S(1)}, u32[]{:S(2)}, u32[]{:S(2)}) collective-permute-start(bf16[64,512]{1,0:T(8,128)(2,1)S(1)} %slice_bitcast_fusion.2), channel_id=1, source_target_pairs={{0,16},{16,0},{32,48},{48,32},{64,80},{80,64},{96,112},{112,96},{1... | collective-permute-start | bytes 196616 | tf_op jit(solution)/shard_map/ppermute | solution.py:323
  71.9 1.4 %collective-permute-start.13 = (bf16[64,512]{1,0:T(8,128)(2,1)S(1)}, bf16[64,512]{1,0:T(8,128)(2,1)S(1)}, u32[]{:S(2)}, u32[]{:S(2)}) collective-permute-start(bf16[64,512]{1,0:T(8,128)(2,1)S(1)} %slice_bitcast_fusion.1), channel_id=1, source_target_pairs={{0,16},{16,0},{32,48},{48,32},{64,80},{80,64},{96,112},{112,96},{1... | collective-permute-start | bytes 196616 | tf_op jit(solution)/shard_map/ppermute | solution.py:323
  72.4 1.3 %collective-permute-start.14 = (bf16[64,512]{1,0:T(8,128)(2,1)S(1)}, bf16[64,512]{1,0:T(8,128)(2,1)S(1)}, u32[]{:S(2)}, u32[]{:S(2)}) collective-permute-start(bf16[64,512]{1,0:T(8,128)(2,1)S(1)} %slice_bitcast_fusion), channel_id=1, source_target_pairs={{0,16},{16,0},{32,48},{48,32},{64,80},{80,64},{96,112},{112,96},{1... | collective-permute-start | bytes 196616 | tf_op jit(solution)/shard_map/ppermute | solution.py:323

commit v4 on v3

--- a/solution.py
+++ b/solution.py
@@ -10,7 +10,7 @@
 
 
 LANES = 128
-ORDER = ((1, 7), (2, 6), (3, 5), (4, 0))
+ORDER = ((2, 6), (4, 0), (3, 5), (1, 7))
 
 
 def spec(block=None, index=None):
@@ -236,8 +236,13 @@
 
 
 def series_kernel(*refs, chips, steps, scale):
-    own, swapped = refs[:chips], refs[chips : 2 * chips]
-    initial, mutes, taper, focusing, partial, spectra, signal, weighted, total = refs[2 * chips :]
+    groups = len(ORDER)
+    own = refs[:chips]
+    swapped = [None] * chips
+    for group, distances in zip(refs[chips : chips + groups], ORDER):
+        for n, d in enumerate(distances):
+            swapped[d] = group.at[n]
+    initial, mutes, taper, focusing, partial, spectra, signal, weighted, total = refs[chips + groups :]
     step = pl.program_id(0)
     me = lax.axis_index("freq")
     chip, core = lax.div(me, 2), lax.rem(me, 2)
@@ -285,7 +290,7 @@
         partial[...] = (total[...] * scale).astype(jnp.bfloat16)
 
 
-def series_update(own, swapped, initial, mutes, taper, scale, rows=16):
+def series_update(own, swapped, initial, mutes, taper, scale, rows=64):
     chips = len(own)
     _, trace, sub, focal = initial.shape
     steps = sub // rows
@@ -294,7 +299,7 @@
         functools.partial(series_kernel, chips=chips, steps=steps, scale=scale),
         grid=(steps,),
         in_specs=[spec((None, rows, 2 * focal), lambda s: (0, s, 0))] * chips
-        + [spec((rows, 2 * focal), lambda s: (s, 0))] * chips
+        + [spec((block.shape[0], rows, 2 * focal), lambda s: (0, s, 0)) for block in swapped]
         + [
             times,
             spec((None, rows, focal), lambda s: (0, s, 0)),
@@ -317,6 +322,24 @@
         compiler_params=pltpu.CompilerParams(vmem_limit_bytes=14 << 20),
         name="series",
     )(*own, *swapped, initial, mutes, taper)
+
+
+def second_kernel(*refs):
+    for n, ref in enumerate(refs[:-1]):
+        refs[-1][n] = ref[1]
+
+
+def second_parts(blocks):
+    shape = (len(blocks),) + blocks[0].shape[1:]
+    return pl.pallas_call(
+        second_kernel,
+        in_specs=[spec()] * len(blocks),
+        out_specs=spec(),
+        out_shape=jax.ShapeDtypeStruct(shape, blocks[0].dtype),
+        cost_estimate=pl.CostEstimate(flops=0, bytes_accessed=1 << 18, transcendentals=0),
+        compiler_params=pltpu.CompilerParams(vmem_limit_bytes=2 << 20),
+        name="second",
+    )(*blocks)
 
 
 def swap_cores(values, freq_count):
@@ -339,12 +362,12 @@
     coeffs = moments(ranks[0, :, 0], tile_mask[0, :, 0], focal_field[0], v_factors[0])
     received = lax.all_to_all(coeffs, "tile", split_axis=0, concat_axis=0, tiled=True)
     terms = rank_terms(received, 1.0 / math.sqrt(freq_count))
-    own, swapped = [None] * chips, [None] * chips
+    own, swapped = [None] * chips, []
     for n, distances in enumerate(ORDER):
         blocks = fields(terms, u_rows[n], distances)
         for d, block in zip(distances, blocks):
             own[d] = shift_chips(block, d, freq_count) if d else block
-            swapped[d] = swap_cores(own[d][1], freq_count)
+        swapped.append(swap_cores(second_parts([own[d] for d in distances]), freq_count))
     trace_length, group_rows = initial_focus.shape[1:3]
     normalizer = 1.0 / float(tile_count * trace_length * group_rows)
     focusing, partial = series_update(

time: 89.1 us -> 81 us (0.909)
  starting transfers between devices: 43.6 us -> 37.7 us
  waiting for transfers between devices: 6 us -> 5.06 us
    ppermute x8 -> x4, starting transfers between devices: 19.2 us -> 12.3 us  [swap_cores(): return lax.ppermute(values, 'freq', [(f, f ^ 1) for f in range(freq_count)])]
    ppermute x7, starting transfers between devices: 16.8 us -> 17.8 us  [shift_chips(): return lax.ppermute(values, 'freq', pairs)]
  transfers between devices with their start and end apart: 16 -> 12, of which waited for: 7 -> 3; matrix products, arithmetic and copies ran while one was open for 1% -> 1% of each run, Pallas kernels for 15% -> 17%
where the time goes in v4:
time: 81 us; the launch traced here: 80.3 us
  starting transfers between devices  37.7 us (47%)
  Pallas kernels  23.9 us (30%)
  blocking collectives  10.2 us (13%)
  waiting for transfers between devices  5.06 us (6%)
  local copies, waits for them, and re-layouts  1.34 us (2%)
  other arithmetic  1.3 us (2%)
  between operations  0.81 us (1%)
    ppermute x7, starting transfers between devices, shift_chips(): return lax.ppermute(values, 'freq', pairs)  17.8 us
    ppermute x4, starting transfers between devices, swap_cores(): return lax.ppermute(values, 'freq', [(f, f ^ 1) for f in range(freq_count)])  12.3 us
    pallas_call x4, Pallas kernels, flatten(): pl.pallas_call(flatten_kernel, grid_spec=pltpu.PrefetchScalarGridSpec(num...  11.3 us
    all_to_all x1, blocking collectives, update(): lax.all_to_all(partial, 'tile', split_axis=0, concat_axis=0, tiled=True)  10.2 us
    all_to_all x1, starting transfers between devices, update(): lax.all_to_all(coeffs, 'tile', split_axis=0, concat_axis=0, tiled=True)  7.58 us
    pallas_call x1, Pallas kernels, moments(): pl.pallas_call(moments_kernel, in_specs=[pl.BlockSpec(memory_space=pltpu....  6.48 us
    all_to_all x1, waiting for transfers between devices, update(): lax.all_to_all(coeffs, 'tile', split_axis=0, concat_axis=0, tiled=True)  4.06 us
    pallas_call x4, Pallas kernels, fields(): pl.pallas_call(fields_kernel, in_specs=[spec(), spec()], out_specs=[spec(...  2.95 us
  transfers between devices with their start and end apart: 12, of which 3 were waited for; matrix products, arithmetic and copies ran while one was open for 1% of the time, Pallas kernels for 17%

profile of v4, /device:TPU:1, one launch (start us, length us, event | category | flops | bytes accessed | tf_op | source)
XLA Modules:
  0.0 80.3 jit_solution(4370392163039340710)
XLA Ops:
  0.6 6.5 %moments.1 = bf16[16,256,128]{2,1,0:T(8,128)(2,1)} custom-call(s32[16]{0:T(128)} %bitcast.19, s32[16]{0:T(128)} %bitcast.20, bf16[1024,2,256]{2,1,0:T(2,128)(2,1)} %bitcast.18, bf16[16,1024,128]{2,1,0:T(8,128)(2,1)} %bitcast.17), custom_call_target="tpu_custom_call" | custom-call | flops 2147483648 | bytes 6291456 | tf_op jit(solution)/shard_map/moments/pallas_call | solution.py:73
  7.1 7.6 %all-to-all-start = ((bf16[16,256,128]{2,1,0:T(8,128)(2,1)}), bf16[16,256,128]{2,1,0:T(8,128)(2,1)S(1)}, u32[]{:S(2)}, u32[]{:S(2)}) async-start(bf16[16,256,128]{2,1,0:T(8,128)(2,1)} %moments.1), calls=%async_computation | async-start | bytes 2097152 | tf_op jit(solution)/shard_map/all_to_all | solution.py:363
  14.7 0.7 pad_add_fusion.place
  15.4 2.8 %shard_map.95.u_rows = bf16[256,2048]{1,0:T(8,128)(2,1)} custom-call(s32[2]{0:T(128)} %pad_add_fusion.place, bf16[1024,16,128]{2,1,0:T(8,128)(2,1)} %bitcast.11), custom_call_target="tpu_custom_call" | custom-call | flops 4194304 | bytes 8388608 | tf_op jit(solution)/shard_map/pallas_call | solution.py:110
  18.2 2.8 %shard_map.97.u_rows = bf16[256,2048]{1,0:T(8,128)(2,1)} custom-call(s32[2]{0:T(128)} %pad_add_fusion.place, bf16[1024,16,128]{2,1,0:T(8,128)(2,1)} %bitcast.12), custom_call_target="tpu_custom_call" | custom-call | flops 4194304 | bytes 8388608 | tf_op jit(solution)/shard_map/pallas_call | solution.py:110
  21.0 2.8 %shard_map.99.u_rows = bf16[256,2048]{1,0:T(8,128)(2,1)} custom-call(s32[2]{0:T(128)} %pad_add_fusion.place, bf16[1024,16,128]{2,1,0:T(8,128)(2,1)} %bitcast.13), custom_call_target="tpu_custom_call" | custom-call | flops 4194304 | bytes 8388608 | tf_op jit(solution)/shard_map/pallas_call | solution.py:110
  23.9 2.8 %shard_map.101.u_rows = bf16[256,2048]{1,0:T(8,128)(2,1)} custom-call(s32[2]{0:T(128)} %pad_add_fusion.place, bf16[1024,16,128]{2,1,0:T(8,128)(2,1)} %bitcast.14), custom_call_target="tpu_custom_call" | custom-call | flops 4194304 | bytes 8388608 | tf_op jit(solution)/shard_map/pallas_call | solution.py:110
  26.7 0.0 copy-start.2
  26.7 0.0 copy-start.1
  26.7 4.1 %all-to-all-done.received = bf16[16,256,128]{2,1,0:T(8,128)(2,1)S(1)} async-done(((bf16[16,256,128]{2,1,0:T(8,128)(2,1)}), bf16[16,256,128]{2,1,0:T(8,128)(2,1)S(1)}, u32[]{:S(2)}, u32[]{:S(2)}) %all-to-all-start) | async-done | bytes 1048608 | tf_op jit(solution)/shard_map/all_to_all | solution.py:363
  30.7 0.5 terms.1
  31.2 0.0 copy-start.3
  31.3 1.2 %copy-done.3 = bf16[256,2048]{1,0:T(8,128)(2,1)S(1)} copy-done((bf16[256,2048]{1,0:T(8,128)(2,1)S(1)}, bf16[256,2048]{1,0:T(8,128)(2,1)}, u32[]{:S(2)}) %copy-start.3) | copy-done | bytes 1048600
  32.5 0.0 copy-start
  32.5 0.7 shard_map.100
  33.2 3.1 %collective-permute-start.1 = (bf16[2,64,512]{2,1,0:T(8,128)(2,1)S(1)}, bf16[2,64,512]{2,1,0:T(8,128)(2,1)S(1)}, u32[]{:S(2)}, u32[]{:S(2)}) collective-permute-start(bf16[2,64,512]{2,1,0:T(8,128)(2,1)S(1)} %get-tuple-element.14), channel_id=1, source_target_pairs={{0,64},{16,80},{32,96},{48,112},{64,128},{80,144},{96,160},{112,17... | collective-permute-start | bytes 393224 | tf_op jit(solution)/shard_map/ppermute | solution.py:351
  36.3 3.1 %collective-permute-start.5 = (bf16[2,64,512]{2,1,0:T(8,128)(2,1)S(1)}, bf16[2,64,512]{2,1,0:T(8,128)(2,1)S(1)}, u32[]{:S(2)}, u32[]{:S(2)}) collective-permute-start(bf16[2,64,512]{2,1,0:T(8,128)(2,1)S(1)} %get-tuple-element.18), channel_id=1, source_target_pairs={{0,192},{16,208},{32,224},{48,240},{64,0},{80,16},{96,32},{112,48}... | collective-permute-start | bytes 393224 | tf_op jit(solution)/shard_map/ppermute | solution.py:351
  39.4 0.0 copy-done.2
  39.4 0.7 shard_map.96
  40.2 0.0 copy-done.1
  40.2 0.0 copy-start.6
  40.2 0.0 copy-start.4
  40.2 0.0 copy-start.5
  40.2 0.7 shard_map.98
  41.0 0.0 copy-done
  41.0 0.7 shard_map.102
  41.7 4.5 %collective-permute-start.3 = (bf16[2,64,512]{2,1,0:T(8,128)(2,1)S(1)}, bf16[2,64,512]{2,1,0:T(8,128)(2,1)S(1)}, u32[]{:S(2)}, u32[]{:S(2)}) collective-permute-start(bf16[2,64,512]{2,1,0:T(8,128)(2,1)S(1)} %get-tuple-element.16), channel_id=1, source_target_pairs={{0,128},{16,144},{32,160},{48,176},{64,192},{80,208},{96,224},{112... | collective-permute-start | bytes 393224 | tf_op jit(solution)/shard_map/ppermute | solution.py:351
  46.2 0.4 collective-permute-start.2
  46.6 4.0 %collective-permute-start.4 = (bf16[2,64,512]{2,1,0:T(8,128)(2,1)S(1)}, bf16[2,64,512]{2,1,0:T(8,128)(2,1)S(1)}, u32[]{:S(2)}, u32[]{:S(2)}) collective-permute-start(bf16[2,64,512]{2,1,0:T(8,128)(2,1)S(1)} %get-tuple-element.17), channel_id=1, source_target_pairs={{0,160},{16,176},{32,192},{48,208},{64,224},{80,240},{96,0},{112,1... | collective-permute-start | bytes 393224 | tf_op jit(solution)/shard_map/ppermute | solution.py:351
  50.6 0.0 collective-permute-done.1.refs_0_.refs_2_
  50.6 0.7 collective-permute-start
  51.4 0.0 collective-permute-done.5.refs_1_.refs_6_
  51.4 1.9 %collective-permute-start.6 = (bf16[2,64,512]{2,1,0:T(8,128)(2,1)S(1)}, bf16[2,64,512]{2,1,0:T(8,128)(2,1)S(1)}, u32[]{:S(2)}, u32[]{:S(2)}) collective-permute-start(bf16[2,64,512]{2,1,0:T(8,128)(2,1)S(1)} %get-tuple-element.19), channel_id=1, source_target_pairs={{0,224},{16,240},{32,0},{48,16},{64,32},{80,48},{96,64},{112,80},{... | collective-permute-start | bytes 393224 | tf_op jit(solution)/shard_map/ppermute | solution.py:351
  53.3 0.0 collective-permute-done.3.refs_0_.refs_4_
  53.3 6.7 %collective-permute-start.7 = (bf16[2,64,512]{2,1,0:T(8,128)(2,1)S(1)}, bf16[2,64,512]{2,1,0:T(8,128)(2,1)S(1)}, u32[]{:S(2)}, u32[]{:S(2)}) collective-permute-start(bf16[2,64,512]{2,1,0:T(8,128)(2,1)S(1)} %second.4), channel_id=1, source_target_pairs={{0,16},{16,0},{32,48},{48,32},{64,80},{80,64},{96,112},{112,96},{1... | collective-permute-start | bytes 393224 | tf_op jit(solution)/shard_map/ppermute | solution.py:346
  60.0 0.0 collective-permute-done.2.refs_0_.refs_3_
  60.0 4.1 %collective-permute-start.8 = (bf16[2,64,512]{2,1,0:T(8,128)(2,1)S(1)}, bf16[2,64,512]{2,1,0:T(8,128)(2,1)S(1)}, u32[]{:S(2)}, u32[]{:S(2)}) collective-permute-start(bf16[2,64,512]{2,1,0:T(8,128)(2,1)S(1)} %second.5), channel_id=1, source_target_pairs={{0,16},{16,0},{32,48},{48,32},{64,80},{80,64},{96,112},{112,96},{1... | collective-permute-start | bytes 393224 | tf_op jit(solution)/shard_map/ppermute | solution.py:346
  64.1 0.0 collective-permute-done.4.refs_1_.refs_5_
  64.1 0.1 collective-permute-start.9
  64.2 0.1 collective-permute-done.refs_0_.refs_1_
  64.4 0.0 collective-permute-done.6.refs_1_.refs_7_
  64.4 1.4 %collective-permute-start.10 = (bf16[2,64,512]{2,1,0:T(8,128)(2,1)S(1)}, bf16[2,64,512]{2,1,0:T(8,128)(2,1)S(1)}, u32[]{:S(2)}, u32[]{:S(2)}) collective-permute-start(bf16[2,64,512]{2,1,0:T(8,128)(2,1)S(1)} %second.7), channel_id=1, source_target_pairs={{0,16},{16,0},{32,48},{48,32},{64,80},{80,64},{96,112},{112,96},{1... | collective-permute-start | bytes 393224 | tf_op jit(solution)/shard_map/ppermute | solution.py:346
  65.8 0.0 copy-done.6
  65.8 0.1 copy.10.refs_14_
  65.9 0.0 collective-permute-done.7.refs_8_
  65.9 0.0 collective-permute-done.8.refs_9_
  65.9 0.0 collective-permute-done.9.refs_10_
  65.9 0.9 %collective-permute-done.10.refs_11_ = bf16[2,64,512]{2,1,0:T(8,128)(2,1)S(1)} collective-permute-done((bf16[2,64,512]{2,1,0:T(8,128)(2,1)S(1)}, bf16[2,64,512]{2,1,0:T(8,128)(2,1)S(1)}, u32[]{:S(2)}, u32[]{:S(2)}) %collective-permute-start.10) | collective-permute-done | bytes 131104 | tf_op jit(solution)/shard_map/ppermute | solution.py:346
  66.8 0.0 copy-done.4
  66.8 0.0 copy-done.5
  66.8 2.6 %series.1 = (bf16[1,32,64,256]{3,2,1,0:T(8,128)(2,1)}, bf16[256,256]{1,0:T(8,128)(2,1)S(1)}) custom-call(bf16[2,64,512]{2,1,0:T(8,128)(2,1)S(1)} %get-tuple-element.12.refs_1_.refs_0_, bf16[2,64,512]{2,1,0:T(8,128)(2,1)S(1)} %collective-permute-done.refs_0_.refs_1_, bf16[2,64,512]{2,1,0:T(8,128)(2,1)S(1)} %collective-permute-done.1.refs_0_.refs_2_, ...), custom_call_target="tpu_custom_call" | custom-call | flops 268435456 | bytes 4194304 | tf_op jit(solution)/shard_map/series/pallas_call | solution.py:298
  69.4 10.2 %all_to_all.14 = bf16[16,16,256]{2,1,0:T(8,128)(2,1)S(1)} all-to-all(bf16[16,16,256]{2,1,0:T(8,128)(2,1)S(1)} %bitcast.10), channel_id=1, replica_groups=mesh['freq'=16,'tile'=16] {'tile'}, dimensions={0} | all-to-all | bytes 262144 | tf_op jit(solution)/shard_map/all_to_all | solution.py:376
  79.6 0.6 convert_reduce_fusion
  (4 shorter events, 0.0 us)
Async XLA Ops:
  7.1 23.6 %all-to-all-start = ((bf16[16,256,128]{2,1,0:T(8,128)(2,1)}), bf16[16,256,128]{2,1,0:T(8,128)(2,1)S(1)}, u32[]{:S(2)}, u32[]{:S(2)}) async-start(bf16[16,256,128]{2,1,0:T(8,128)(2,1)} %moments.1), calls=%async_computation | async-start | bytes 2097152 | tf_op jit(solution)/shard_map/all_to_all | solution.py:363
  26.7 12.7 %copy-start.2 = (bf16[256,2048]{1,0:T(8,128)(2,1)S(1)}, bf16[256,2048]{1,0:T(8,128)(2,1)}, u32[]{:S(2)}) copy-start(bf16[256,2048]{1,0:T(8,128)(2,1)} %shard_map.95.u_rows) | copy-start | bytes 3145732
  26.7 13.5 %copy-start.1 = (bf16[256,2048]{1,0:T(8,128)(2,1)S(1)}, bf16[256,2048]{1,0:T(8,128)(2,1)}, u32[]{:S(2)}) copy-start(bf16[256,2048]{1,0:T(8,128)(2,1)} %shard_map.97.u_rows) | copy-start | bytes 3145732
  31.2 1.2 %copy-start.3 = (bf16[256,2048]{1,0:T(8,128)(2,1)S(1)}, bf16[256,2048]{1,0:T(8,128)(2,1)}, u32[]{:S(2)}) copy-start(bf16[256,2048]{1,0:T(8,128)(2,1)} %shard_map.99.u_rows) | copy-start | bytes 3145732
  32.5 8.5 %copy-start = (bf16[256,2048]{1,0:T(8,128)(2,1)S(1)}, bf16[256,2048]{1,0:T(8,128)(2,1)}, u32[]{:S(2)}) copy-start(bf16[256,2048]{1,0:T(8,128)(2,1)} %shard_map.101.u_rows) | copy-start | bytes 3145732
  33.2 17.4 %collective-permute-start.1 = (bf16[2,64,512]{2,1,0:T(8,128)(2,1)S(1)}, bf16[2,64,512]{2,1,0:T(8,128)(2,1)S(1)}, u32[]{:S(2)}, u32[]{:S(2)}) collective-permute-start(bf16[2,64,512]{2,1,0:T(8,128)(2,1)S(1)} %get-tuple-element.14), channel_id=1, source_target_pairs={{0,64},{16,80},{32,96},{48,112},{64,128},{80,144},{96,160},{112,17... | collective-permute-start | bytes 393224 | tf_op jit(solution)/shard_map/ppermute | solution.py:351
  36.3 15.1 %collective-permute-start.5 = (bf16[2,64,512]{2,1,0:T(8,128)(2,1)S(1)}, bf16[2,64,512]{2,1,0:T(8,128)(2,1)S(1)}, u32[]{:S(2)}, u32[]{:S(2)}) collective-permute-start(bf16[2,64,512]{2,1,0:T(8,128)(2,1)S(1)} %get-tuple-element.18), channel_id=1, source_target_pairs={{0,192},{16,208},{32,224},{48,240},{64,0},{80,16},{96,32},{112,48}... | collective-permute-start | bytes 393224 | tf_op jit(solution)/shard_map/ppermute | solution.py:351
  40.2 25.6 %copy-start.6 = (f32[1,64]{1,0:T(1,128)S(1)}, f32[1,64]{1,0:T(1,128)}, u32[]{:S(2)}) copy-start(f32[1,64]{1,0:T(1,128)} %param.15) | copy-start | bytes 772
  40.2 26.6 %copy-start.4 = (bf16[1,32,64,256]{3,2,1,0:T(8,128)(2,1)S(1)}, bf16[1,32,64,256]{3,2,1,0:T(8,128)(2,1)}, u32[]{:S(2)}) copy-start(bf16[1,32,64,256]{3,2,1,0:T(8,128)(2,1)} %refs_12_.1) | copy-start | bytes 3145732
  40.2 26.6 %copy-start.5 = (s32[1,64,256]{2,1,0:T(8,128)S(1)}, s32[1,64,256]{2,1,0:T(8,128)}, u32[]{:S(2)}) copy-start(s32[1,64,256]{2,1,0:T(8,128)} %refs_13_.1) | copy-start | bytes 196612
  41.7 11.6 %collective-permute-start.3 = (bf16[2,64,512]{2,1,0:T(8,128)(2,1)S(1)}, bf16[2,64,512]{2,1,0:T(8,128)(2,1)S(1)}, u32[]{:S(2)}, u32[]{:S(2)}) collective-permute-start(bf16[2,64,512]{2,1,0:T(8,128)(2,1)S(1)} %get-tuple-element.16), channel_id=1, source_target_pairs={{0,128},{16,144},{32,160},{48,176},{64,192},{80,208},{96,224},{112... | collective-permute-start | bytes 393224 | tf_op jit(solution)/shard_map/ppermute | solution.py:351
  46.2 13.9 %collective-permute-start.2 = (bf16[2,64,512]{2,1,0:T(8,128)(2,1)S(1)}, bf16[2,64,512]{2,1,0:T(8,128)(2,1)S(1)}, u32[]{:S(2)}, u32[]{:S(2)}) collective-permute-start(bf16[2,64,512]{2,1,0:T(8,128)(2,1)S(1)} %get-tuple-element.15), channel_id=1, source_target_pairs={{0,96},{16,112},{32,128},{48,144},{64,160},{80,176},{96,192},{112,... | collective-permute-start | bytes 393224 | tf_op jit(solution)/shard_map/ppermute | solution.py:351
  46.6 17.5 %collective-permute-start.4 = (bf16[2,64,512]{2,1,0:T(8,128)(2,1)S(1)}, bf16[2,64,512]{2,1,0:T(8,128)(2,1)S(1)}, u32[]{:S(2)}, u32[]{:S(2)}) collective-permute-start(bf16[2,64,512]{2,1,0:T(8,128)(2,1)S(1)} %get-tuple-element.17), channel_id=1, source_target_pairs={{0,160},{16,176},{32,192},{48,208},{64,224},{80,240},{96,0},{112,1... | collective-permute-start | bytes 393224 | tf_op jit(solution)/shard_map/ppermute | solution.py:351
  50.6 13.7 %collective-permute-start = (bf16[2,64,512]{2,1,0:T(8,128)(2,1)S(1)}, bf16[2,64,512]{2,1,0:T(8,128)(2,1)S(1)}, u32[]{:S(2)}, u32[]{:S(2)}) collective-permute-start(bf16[2,64,512]{2,1,0:T(8,128)(2,1)S(1)} %get-tuple-element.13), channel_id=1, source_target_pairs={{0,32},{16,48},{32,64},{48,80},{64,96},{80,112},{96,128},{112,144}... | collective-permute-start | bytes 393224 | tf_op jit(solution)/shard_map/ppermute | solution.py:351
  51.4 13.0 %collective-permute-start.6 = (bf16[2,64,512]{2,1,0:T(8,128)(2,1)S(1)}, bf16[2,64,512]{2,1,0:T(8,128)(2,1)S(1)}, u32[]{:S(2)}, u32[]{:S(2)}) collective-permute-start(bf16[2,64,512]{2,1,0:T(8,128)(2,1)S(1)} %get-tuple-element.19), channel_id=1, source_target_pairs={{0,224},{16,240},{32,0},{48,16},{64,32},{80,48},{96,64},{112,80},{... | collective-permute-start | bytes 393224 | tf_op jit(solution)/shard_map/ppermute | solution.py:351
  53.3 12.6 %collective-permute-start.7 = (bf16[2,64,512]{2,1,0:T(8,128)(2,1)S(1)}, bf16[2,64,512]{2,1,0:T(8,128)(2,1)S(1)}, u32[]{:S(2)}, u32[]{:S(2)}) collective-permute-start(bf16[2,64,512]{2,1,0:T(8,128)(2,1)S(1)} %second.4), channel_id=1, source_target_pairs={{0,16},{16,0},{32,48},{48,32},{64,80},{80,64},{96,112},{112,96},{1... | collective-permute-start | bytes 393224 | tf_op jit(solution)/shard_map/ppermute | solution.py:346
  60.0 5.9 %collective-permute-start.8 = (bf16[2,64,512]{2,1,0:T(8,128)(2,1)S(1)}, bf16[2,64,512]{2,1,0:T(8,128)(2,1)S(1)}, u32[]{:S(2)}, u32[]{:S(2)}) collective-permute-start(bf16[2,64,512]{2,1,0:T(8,128)(2,1)S(1)} %second.5), channel_id=1, source_target_pairs={{0,16},{16,0},{32,48},{48,32},{64,80},{80,64},{96,112},{112,96},{1... | collective-permute-start | bytes 393224 | tf_op jit(solution)/shard_map/ppermute | solution.py:346
  64.1 1.8 %collective-permute-start.9 = (bf16[2,64,512]{2,1,0:T(8,128)(2,1)S(1)}, bf16[2,64,512]{2,1,0:T(8,128)(2,1)S(1)}, u32[]{:S(2)}, u32[]{:S(2)}) collective-permute-start(bf16[2,64,512]{2,1,0:T(8,128)(2,1)S(1)} %second.6), channel_id=1, source_target_pairs={{0,16},{16,0},{32,48},{48,32},{64,80},{80,64},{96,112},{112,96},{1... | collective-permute-start | bytes 393224 | tf_op jit(solution)/shard_map/ppermute | solution.py:346
  64.4 2.4 %collective-permute-start.10 = (bf16[2,64,512]{2,1,0:T(8,128)(2,1)S(1)}, bf16[2,64,512]{2,1,0:T(8,128)(2,1)S(1)}, u32[]{:S(2)}, u32[]{:S(2)}) collective-permute-start(bf16[2,64,512]{2,1,0:T(8,128)(2,1)S(1)} %second.7), channel_id=1, source_target_pairs={{0,16},{16,0},{32,48},{48,32},{64,80},{80,64},{96,112},{112,96},{1... | collective-permute-start | bytes 393224 | tf_op jit(solution)/shard_map/ppermute | solution.py:346
